TPU v7x, 512 devices: a whole 4x8x8 slice. The times are simulated.
512 devices in a mesh: dp: 128 (over y, x, z_lo, core), strip: 4 (over z_hi).
Axes of the slice: x: 4, y: 8, z: 8 (z_hi: 4, z_lo: 2; z = z_hi * 2 + z_lo), core: 2. Of those that a mesh axis runs over, the one named last changes fastest.
Arguments:
- latents: bfloat16 [128, 4, 320, 128], P('dp', 'strip'), may hold values from -6 to 6
- cotangent: bfloat16 [128, 4, 320, 128], P('dp', 'strip'), may hold values from -16 to 16
- weight: bfloat16 [320, 2880], P('strip'), may hold values from -0.109375 to 0.109375
- master: float32 [512, 2880], P('dp'), may hold values from -0.21875 to 0.21875
- first_moment: float32 [512, 2880], P('dp'), may hold values from -6 to 6
- second_moment: float32 [512, 2880], P('dp'), may hold values from 0.005 to 0.05
- owner_list: int32 [320], replicated, may hold values from 0 to 127, as said below
Outputs:
- output: bfloat16 [128, 4, 320, 128], P('dp', 'strip')
- grad_input: bfloat16 [128, 4, 320, 128], P('dp', 'strip')
- new_weight: bfloat16 [320, 2880], P('strip')
- new_master: float32 [512, 2880], P('dp')
- new_first: float32 [512, 2880], P('dp')
- new_second: float32 [512, 2880], P('dp')
Inputs may be any that keep to these rules, and one draw needn't show every extreme that they name: `owner_list`: each of the 128 ranks owns at least one and at most 4 buckets, and some rank owns exactly 4.
All inputs are finite; a program needn't handle non-finite values.
Results may differ from a plain program's by a relative error of at most 0.0033.
Values may be sent and summed in bfloat16 or wider, within the bound.
No kernel may reach another device: no remote copies, remote signals or barrier semaphores. Data moves between devices by JAX's collectives and lax.ppermute only.
A program may use at most 64 MiB of HBM per device.

v0:
```python
import functools
import jax
import jax.numpy as jnp
from jax import lax
from jax.experimental import pallas as pl
from jax.experimental.pallas import tpu as pltpu
from jax.sharding import Mesh, PartitionSpec as P

beta_first = 0.9
beta_second = 0.999
learn_rate = 0.01
epsilon = 1e-08
bias_first = 1.0 - 0.9**10
bias_second = 1.0 - 0.999**10

interpret = False
LANES = 128
RANK_SHAPE = (8, 8, 2)
TERMS = 2
taps = [(dh, dw) for dh in (-1, 0, 1) for dw in (-1, 0, 1)]
f32 = jnp.float32
bf16 = jnp.bfloat16


def call(body, out_shape, scratch=(), scalars=0, inputs=0):
    specs = {}
    if scalars:
        specs["in_specs"] = [pl.BlockSpec(memory_space=pltpu.SMEM)] * scalars + [
            pl.BlockSpec(memory_space=pltpu.VMEM)
        ] * inputs
    return pl.pallas_call(
        body,
        out_shape=out_shape,
        scratch_shapes=scratch,
        interpret=interpret,
        compiler_params=pltpu.CompilerParams(vmem_limit_bytes=20 << 20),
        **specs,
    )


def dot(left, right, left_dim, right_dim):
    return lax.dot_general(
        left, right, (((left_dim,), (right_dim,)), ((), ())), preferred_element_type=f32
    )


def shifted(value):
    lane = lax.broadcasted_iota(jnp.int32, value.shape, 1)
    last = value.shape[1] - 1
    before = jnp.where(lane == 0, 0.0, pltpu.roll(value, 1, 1))
    after = jnp.where(lane == last, 0.0, pltpu.roll(value, last, 1))
    return {-1: before.astype(bf16), 0: value.astype(bf16), 1: after.astype(bf16)}


def fill(cols, rows, load, direction):
    first = load(0)
    count, width = first.shape
    for index, (dh, _) in enumerate(taps):
        for h in range(rows):
            if not 0 <= h + direction * dh < rows:
                cols[index * count : (index + 1) * count, h * width : (h + 1) * width] = jnp.zeros(
                    (count, width), bf16
                )
    for source in range(rows):
        versions = shifted(first if source == 0 else load(source))
        for index, (dh, dw) in enumerate(taps):
            h = source - direction * dh
            if 0 <= h < rows:
                cols[index * count : (index + 1) * count, h * width : (h + 1) * width] = versions[
                    direction * dw
                ]


def activated(gathered, channels, h):
    value = gathered[h, :channels, :].astype(f32)
    return (value / (1.0 + jnp.exp(-value))).astype(bf16).astype(f32)


def pack_body(pixels, upstream, outgoing, arrived):
    strips, channels = outgoing.shape[0], pixels.shape[0]
    copies = []
    for strip in range(strips):
        copies.append((pixels, outgoing.at[strip, :channels, :]))
        copies.append((upstream.at[strip], outgoing.at[strip, channels:, :]))
    copies = [
        pltpu.make_async_copy(source, target, arrived.at[index])
        for index, (source, target) in enumerate(copies)
    ]
    for copy in copies:
        copy.start()
    for copy in copies:
        copy.wait()


def split_body(strip, master, first_moment, second_moment, pieces, *, strips, step):
    state = jnp.concatenate([master[...], first_moment[...], second_moment[...]], axis=0)
    terms = []
    for _ in range(TERMS):
        term = state.astype(bf16).astype(f32)
        terms.append(term)
        state = state - term
    terms = jnp.concatenate(terms, axis=0)
    share = terms.shape[0] // strips
    mine = terms[:share]
    for other in range(1, strips):
        mine = jnp.where(strip[0] == other, terms[other * share : (other + 1) * share], mine)
    groups, height, padded = pieces.shape
    excess = (groups - 1) * step + padded - mine.shape[1]
    mine = jnp.concatenate([mine, jnp.zeros((share, excess), f32)], axis=1)
    mine = jnp.concatenate([mine, jnp.zeros((height - share, mine.shape[1]), f32)], axis=0)
    for group in range(groups):
        pieces[group] = mine[:, group * step : group * step + padded].astype(bf16)


def gradient_body(gathered, pieces, grads, cols, *, channels, step):
    rows = gathered.shape[0]
    quarter = gathered.shape[1] - channels
    fill(cols, rows, functools.partial(activated, gathered, channels), 1)
    whole = len(taps) * channels
    if cols.shape[0] > whole:
        cols[whole:, :] = jnp.zeros((cols.shape[0] - whole, cols.shape[1]), bf16)
    upstream = jnp.concatenate([gathered[h, channels:, :] for h in range(rows)], axis=1)
    groups, _, padded = grads.shape
    for group in range(groups):
        product = dot(upstream, cols[group * step : group * step + padded, :], 1, 1)
        grads[group, :quarter, :] = product.astype(bf16)
        grads[group, quarter:, :] = pieces[group]


def convolution_body(
    strip, gathered, residual, weight, turned, *results, channels
):
    *results, cols, back_cols, whole = results
    rows, quarter, width = residual.shape
    fill(cols, rows, functools.partial(activated, gathered, channels), 1)
    convolved = dot(weight[...], cols[...], 1, 0)
    for h in range(rows):
        whole[h, :quarter, :] = (
            residual[h].astype(f32) + convolved[:, h * width : (h + 1) * width]
        ).astype(bf16)
    fill(back_cols, rows, lambda h: gathered[h, channels:, :].astype(f32), -1)
    spread = dot(turned[...], back_cols[...], 1, 0)
    for h in range(rows):
        whole[h, quarter:, :] = spread[:, h * width : (h + 1) * width].astype(bf16)
    for ahead, result in enumerate(results):
        target = strip[0] + ahead
        result[...] = whole[jnp.where(target >= rows, target - rows, target)]


def collect_body(strip, pixels, upstream, *pieces, quarter):
    *pieces, output, grad_input = pieces
    strips = len(pieces)
    spread = jnp.zeros(pixels.shape, f32)
    for behind, piece in enumerate(pieces):
        source = strip[0] - behind
        source = jnp.where(source < 0, source + strips, source)
        output[pl.ds(pl.multiple_of(source * quarter, quarter), quarter), :] = piece[:quarter, :]
        spread = spread + piece[quarter:, :].astype(f32)
    value = pixels[...].astype(f32)
    sigmoid = 1.0 / (1.0 + jnp.exp(-value))
    derivative = sigmoid * (1.0 + value * (1.0 - sigmoid))
    grad_input[...] = (upstream[...].astype(f32) + spread * derivative).astype(bf16)


def turn_body(received, message, *, quarter, share):
    groups, _, padded = received.shape
    values = [received[group].astype(f32) for group in range(groups)]
    total = values[0][:quarter]
    for value in values[1:]:
        total = total + value[:quarter]
    rows = [total] + [value[quarter : quarter + share] for value in values]
    spare = LANES - quarter - groups * share
    if spare:
        rows.append(jnp.zeros((spare, padded), f32))
    turned = jnp.transpose(jnp.concatenate(rows, axis=0))
    parts, strips, chunk, _ = message.shape
    for part in range(parts):
        piece = turned[part * chunk : (part + 1) * chunk, :].astype(bf16)
        for strip in range(strips):
            message[part, strip] = piece


def adam(grads, master, first_moment, second_moment):
    first_new = beta_first * first_moment + (1.0 - beta_first) * grads
    second_new = beta_second * second_moment + (1.0 - beta_second) * grads * grads
    update = learn_rate * (first_new / bias_first) / (jnp.sqrt(second_new / bias_second) + epsilon)
    return master - update, first_new, second_new


def publish_body(
    strip, received, slots, message, *, quarter, capacity, share, groups, cores, root
):
    pairs, chunk, _ = received.shape
    strips = slots.shape[0]
    parts = pairs // strips
    chips = message.shape[0]
    columns = max(LANES, chips * cores * capacity)
    mine = slots[0:1, :]
    for other in range(1, strips):
        mine = jnp.where(strip[0] == other, slots[other : other + 1, :], mine)
    wide = jnp.concatenate([mine] * 3, axis=1)
    owner, place = wide // capacity, wide % capacity
    owner_part = owner // (groups * cores) * cores + owner % cores
    owner_group = owner // cores % groups
    row = lax.broadcasted_iota(jnp.int32, (LANES, 3 * LANES), 0) - quarter
    array = lax.broadcasted_iota(jnp.int32, (LANES, 3 * LANES), 1) // LANES
    usable = (row >= 0) & (row < groups * share) & (row // share == owner_group) & (wide >= 0)
    index = lax.broadcasted_iota(jnp.int32, (columns, LANES), 0)
    chosen = jnp.zeros((chunk, columns), f32)
    grads = jnp.zeros((chunk, LANES), f32)
    picked = jnp.zeros((parts * chunk, 3 * LANES), f32)
    for other in range(strips):
        values = [received[part * strips + other].astype(f32) for part in range(parts)]
        total = values[0]
        for value in values[1:]:
            total = total + value
        matches = jnp.where(index == slots[other : other + 1, :], 1.0, 0.0).astype(bf16)
        chosen = chosen + dot(total.astype(bf16), matches, 1, 1)
        grads = jnp.where(strip[0] == other, total, grads)
        place_of = (other * share + row % share) % (3 * capacity)
        here = usable & (place_of // capacity == array) & (place_of % capacity == place)
        here = jnp.where(here, 1.0, 0.0).astype(bf16)
        picked = picked + dot(jnp.concatenate(values, axis=0).astype(bf16), here, 1, 0)
    state = jnp.zeros((chunk, 3 * LANES), f32)
    for part in range(parts):
        state = state + jnp.where(
            owner_part == part, picked[part * chunk : (part + 1) * chunk], 0.0
        )
    fresh, _, _ = adam(
        grads / root, state[:, :LANES], state[:, LANES : 2 * LANES], state[:, 2 * LANES :]
    )
    lane = lax.broadcasted_iota(jnp.int32, (chunk, LANES), 1)
    span = cores * capacity
    per_tile = LANES // span
    for chip in range(chips):
        tile = chosen[:, chip // per_tile * LANES : (chip // per_tile + 1) * LANES]
        shift = (quarter - span * (chip % per_tile)) % LANES
        moved = tile if shift == 0 else pltpu.roll(tile, shift, 1)
        value = jnp.where(lane < quarter, fresh, jnp.where(lane < quarter + span, moved, 0.0))
        message[chip] = value.astype(bf16)


def finish_body(
    core, near, far, master, first_moment, second_moment, filled,
    new_weight, new_master, new_first, new_second, *, groups, step, root,
):
    quarter, capacity = new_weight.shape[0], master.shape[0]
    chips, _, _ = near.shape
    lines = chips // groups
    rows = []
    for group in range(groups):
        block = []
        for line in range(lines):
            ours = near[line * groups + group].astype(f32)
            others = far[line * groups + group].astype(f32)
            block.append(jnp.where(core[0] == 0, ours, others))
            block.append(jnp.where(core[0] == 0, others, ours))
        rows.append(jnp.concatenate(block, axis=0)[:step])
    rows = jnp.concatenate(rows, axis=0).astype(bf16)
    unit = lax.broadcasted_iota(jnp.int32, (LANES, LANES), 0) == lax.broadcasted_iota(
        jnp.int32, (LANES, LANES), 1
    )
    turned = dot(jnp.where(unit, 1.0, 0.0).astype(bf16), rows, 1, 1)
    new_weight[...] = turned[:quarter].astype(bf16)
    low = turned[quarter : quarter + capacity]
    high = turned[quarter + capacity : quarter + 2 * capacity]
    grads = jnp.where(core[0] == 0, low, high) / root
    fresh, first_new, second_new = adam(
        grads, master[...], first_moment[...], second_moment[...]
    )
    keep = filled[...] > 0.0
    new_master[...] = jnp.where(keep, fresh, master[...])
    new_first[...] = jnp.where(keep, first_new, first_moment[...])
    new_second[...] = jnp.where(keep, second_new, second_moment[...])


def slot_tables(owner_list, capacity):
    count = owner_list.shape[0]
    same_owner = owner_list[:, None] == owner_list[None, :]
    order = jnp.arange(count, dtype=jnp.int32)
    earlier = order[None, :] < order[:, None]
    return owner_list * capacity + jnp.sum((same_owner & earlier).astype(jnp.int32), axis=1)


def exchange(value, axes):
    return lax.all_to_all(value, axes, 0, 0, tiled=True)


def local(latents, cotangent, weight, master, first_moment, second_moment, owner_list):
    lines, groups, cores, strips = (lax.axis_size(a) for a in ("line", "group", "core", "strip"))
    parts, chips = lines * cores, lines * groups
    ranks = parts * groups
    strip, core = lax.axis_index("strip"), lax.axis_index("core")
    rank = (lax.axis_index("line") * groups + lax.axis_index("group")) * cores + core
    strip_scalar = strip.reshape(1).astype(jnp.int32)
    channels, width = latents.shape[2:]
    quarter = channels // strips
    capacity = master.shape[0]
    share = TERMS * 3 * capacity // strips
    height = -(-share // 8) * 8
    taken = len(taps) * channels
    step = taken // groups
    padded = -(-step // LANES) * LANES
    chunk = padded // parts
    rows = strips
    root = float(ranks * rows * width) ** 0.5
    pixels, upstream = latents[0, 0], cotangent[0, 0]

    outgoing = pl.pallas_call(
        pack_body,
        out_shape=jax.ShapeDtypeStruct((strips, channels + quarter, width), bf16),
        in_specs=[pl.BlockSpec(memory_space=pl.ANY)] * 2,
        out_specs=pl.BlockSpec(memory_space=pl.ANY),
        scratch_shapes=[pltpu.SemaphoreType.DMA((2 * strips,))],
        name="pack",
        interpret=interpret,
    )(pixels, upstream.reshape(strips, quarter, width))
    gathered = exchange(outgoing, "strip")

    slot_ids = slot_tables(owner_list, capacity)
    slots = jnp.pad(
        slot_ids.reshape(strips, quarter), ((0, 0), (0, LANES - quarter)), constant_values=-1
    )
    owned = jnp.sum((owner_list == rank).astype(jnp.int32))
    filled = (jnp.arange(capacity, dtype=jnp.int32) < owned).astype(f32)[:, None]
    turned = weight.reshape(quarter, len(taps), channels).transpose(2, 1, 0)
    turned = turned.reshape(channels, len(taps) * quarter)
    pieces = call(
        functools.partial(split_body, strips=strips, step=step),
        jax.ShapeDtypeStruct((groups, height, padded), bf16),
        scalars=1,
        inputs=3,
    )(strip_scalar, master, first_moment, second_moment)
    gathered, slots, filled, turned, pieces = lax.optimization_barrier(
        (gathered, slots, filled, turned, pieces)
    )

    grads = call(
        functools.partial(gradient_body, channels=channels, step=step),
        jax.ShapeDtypeStruct((groups, quarter + height, padded), bf16),
        [pltpu.VMEM(((groups - 1) * step + padded, rows * width), bf16)],
    )(gathered, pieces)
    by_group = exchange(grads, "group")

    residual = lax.dynamic_slice_in_dim(gathered, strip * quarter, quarter, axis=1)
    results = call(
        functools.partial(convolution_body, channels=channels),
        [jax.ShapeDtypeStruct((quarter + channels, width), bf16)] * strips,
        [
            pltpu.VMEM((taken, rows * width), bf16),
            pltpu.VMEM((len(taps) * quarter, rows * width), bf16),
            pltpu.VMEM((rows, quarter + channels, width), bf16),
        ],
        scalars=1,
        inputs=4,
    )(strip_scalar, gathered, residual, weight, turned)

    returned = [
        lax.ppermute(result, "strip", [(i, (i + ahead) % strips) for i in range(strips)])
        if ahead
        else result
        for ahead, result in enumerate(results)
    ]

    by_part = call(
        functools.partial(turn_body, quarter=quarter, share=share),
        jax.ShapeDtypeStruct((parts, strips, chunk, LANES), bf16),
    )(by_group)
    by_part = exchange(
        by_part.reshape(parts * strips, chunk, LANES), ("line", "core", "strip")
    )
    message = call(
        functools.partial(
            publish_body, quarter=quarter, capacity=capacity, share=share, groups=groups,
            cores=cores, root=root,
        ),
        jax.ShapeDtypeStruct((chips, chunk, LANES), bf16),
        scalars=1,
        inputs=2,
    )(strip_scalar, by_part, slots)
    near = exchange(message, ("line", "group"))

    near, *returned = lax.optimization_barrier((near, *returned))
    output, grad_input = call(
        functools.partial(collect_body, quarter=quarter),
        [jax.ShapeDtypeStruct((channels, width), bf16)] * 2,
        scalars=1,
        inputs=2 + strips,
    )(strip_scalar, pixels, upstream, *returned)

    far = lax.ppermute(near, "core", [(i, cores - 1 - i) for i in range(cores)])
    new_weight, new_master, new_first, new_second = call(
        functools.partial(finish_body, groups=groups, step=step, root=root),
        [jax.ShapeDtypeStruct((quarter, taken), bf16)]
        + [jax.ShapeDtypeStruct(master.shape, f32)] * 3,
        scalars=1,
        inputs=6,
    )(core.reshape(1).astype(jnp.int32), near, far, master, first_moment, second_moment, filled)
    return (output[None, None], grad_input[None, None], new_weight, new_master, new_first, new_second)


def solution(mesh):
    fine = Mesh(
        mesh.devices.reshape(RANK_SHAPE + (mesh.shape["strip"],)),
        ("line", "group", "core", "strip"),
    )
    ranks = ("line", "group", "core")
    images = P(ranks, "strip", None, None)
    specs = (images, images, P("strip", None), P(ranks, None), P(ranks, None), P(ranks, None))

    return jax.shard_map(
        local, mesh=fine, in_specs=specs + (P(),), out_specs=specs, check_vma=False
    )
```

profile of v0, /device:TPU:1, one launch (start us, length us, event | category | flops | bytes accessed | tf_op | source)
XLA Modules:
  0.0 115.8 jit_solution(7759060796936087443)
XLA Ops:
  0.6 13.6 %pack.1 = bf16[4,400,128]{2,1,0:T(8,128)(2,1)} custom-call(bf16[320,128]{1,0:T(8,128)(2,1)} %bitcast.13, bf16[4,80,128]{2,1,0:T(8,128)(2,1)} %bitcast.15), custom_call_target="tpu_custom_call" | custom-call | tf_op jit(solution)/shard_map/pack/pallas_call | solution.py:309
  14.2 11.0 %all-to-all-start = ((bf16[4,400,128]{2,1,0:T(8,128)(2,1)}), bf16[4,400,128]{2,1,0:T(8,128)(2,1)S(1)}, u32[]{:S(2)}, u32[]{:S(2)}) async-start(bf16[4,400,128]{2,1,0:T(8,128)(2,1)} %pack.1), calls=%async_computation | async-start | bytes 819200 | tf_op jit(solution)/shard_map/all_to_all | solution.py:286
  25.2 0.7 copy-done.6
  25.9 0.2 convert_reduce_fusion
  26.1 0.6 convert_reduce_fusion.1
  26.8 0.1 reshape.43
  26.8 0.4 copy.17
  27.2 0.4 copy.18
  27.6 0.4 copy-done.3
  28.0 0.0 copy-done.4
  28.0 0.0 copy-done.5
  28.1 0.2 shard_map.118.pieces
  28.2 0.6 fusion.1.filled
  28.9 6.5 %all-to-all-done.gathered = bf16[4,400,128]{2,1,0:T(8,128)(2,1)S(1)} async-done(((bf16[4,400,128]{2,1,0:T(8,128)(2,1)}), bf16[4,400,128]{2,1,0:T(8,128)(2,1)S(1)}, u32[]{:S(2)}, u32[]{:S(2)}) %all-to-all-start) | async-done | bytes 409632 | tf_op jit(solution)/shard_map/all_to_all | solution.py:286
  35.3 1.4 %shard_map.119 = bf16[8,88,384]{2,1,0:T(8,128)(2,1)S(1)} custom-call(bf16[4,400,128]{2,1,0:T(8,128)(2,1)S(1)} %all-to-all-done.gathered, bf16[8,8,384]{2,1,0:T(8,128)(2,1)S(1)} %shard_map.118.pieces), custom_call_target="tpu_custom_call" | custom-call | tf_op jit(solution)/shard_map/pallas_call | solution.py:338
  36.7 17.2 %all_to_all.20.received = bf16[8,88,384]{2,1,0:T(8,128)(2,1)S(1)} all-to-all(bf16[8,88,384]{2,1,0:T(8,128)(2,1)S(1)} %shard_map.119), channel_id=1, replica_groups=mesh['line'=8,'group'=8,'core'=2,'strip'=4] {'group'}, dimensions={0} | all-to-all | bytes 1081344 | tf_op jit(solution)/shard_map/all_to_all | solution.py:286
  53.9 0.1 shard_map.120
  54.1 28.0 %all_to_all.21.received = bf16[64,24,128]{2,1,0:T(8,128)(2,1)S(1)} all-to-all(bf16[64,24,128]{2,1,0:T(8,128)(2,1)S(1)} %bitcast.12), channel_id=1, replica_groups=mesh['line'=8,'group'=8,'core'=2,'strip'=4] {'line','core','strip'}, dimensions={0} | all-to-all | bytes 786432 | tf_op jit(solution)/shard_map/all_to_all | solution.py:286
  82.1 1.5 %shard_map.121 = bf16[64,24,128]{2,1,0:T(8,128)(2,1)} custom-call(s32[1]{0:T(128)} %bitcast.strip, bf16[64,24,128]{2,1,0:T(8,128)(2,1)S(1)} %all_to_all.21.received, s32[4,128]{1,0:T(4,128)S(1)} %pad.4.slots), custom_call_target="tpu_custom_call" | custom-call | tf_op jit(solution)/shard_map/pallas_call | solution.py:372
  83.6 5.5 %all-to-all-start.3 = ((bf16[64,24,128]{2,1,0:T(8,128)(2,1)}), bf16[64,24,128]{2,1,0:T(8,128)(2,1)S(1)}, u32[]{:S(2)}, u32[]{:S(2)}) async-start(bf16[64,24,128]{2,1,0:T(8,128)(2,1)} %shard_map.121), calls=%async_computation.3 | async-start | bytes 786432 | tf_op jit(solution)/shard_map/all_to_all | solution.py:286
  89.1 0.2 copy.19.turned
  89.3 1.3 %shard_map.122 = (bf16[400,128]{1,0:T(8,128)(2,1)S(1)}, bf16[400,128]{1,0:T(8,128)(2,1)S(1)}, bf16[400,128]{1,0:T(8,128)(2,1)S(1)}, bf16[400,128]{1,0:T(8,128)(2,1)S(1)}) custom-call(s32[1]{0:T(128)} %bitcast.strip, bf16[4,400,128]{2,1,0:T(8,128)(2,1)S(1)} %all-to-all-done.gathered, bf16[4,80,128]{2,1,0:T(8,128)(2,1)S(1)} %constant_dynamic-slice_fusion.residual, ...), custom_call_target="tpu_custom_call" | custom-call | tf_op jit(solution)/shard_map/pallas_call | solution.py:346
  90.7 2.5 %collective-permute-start = (bf16[400,128]{1,0:T(8,128)(2,1)S(1)}, bf16[400,128]{1,0:T(8,128)(2,1)S(1)}, u32[]{:S(2)}, u32[]{:S(2)}) collective-permute-start(bf16[400,128]{1,0:T(8,128)(2,1)S(1)} %get-tuple-element.31), channel_id=1, source_target_pairs={{0,1},{1,2},{2,3},{3,0},{4,5},{5,6},{6,7},{7,4},{8,9},{9,10},{10,1... | collective-permute-start | bytes 307208 | tf_op jit(solution)/shard_map/ppermute | solution.py:359
  93.2 3.6 %collective-permute-start.1 = (bf16[400,128]{1,0:T(8,128)(2,1)S(1)}, bf16[400,128]{1,0:T(8,128)(2,1)S(1)}, u32[]{:S(2)}, u32[]{:S(2)}) collective-permute-start(bf16[400,128]{1,0:T(8,128)(2,1)S(1)} %get-tuple-element.32), channel_id=1, source_target_pairs={{0,2},{1,3},{2,0},{3,1},{4,6},{5,7},{6,4},{7,5},{8,10},{9,11},{10,... | collective-permute-start | bytes 307208 | tf_op jit(solution)/shard_map/ppermute | solution.py:359
  96.8 4.5 %collective-permute-start.2 = (bf16[400,128]{1,0:T(8,128)(2,1)S(1)}, bf16[400,128]{1,0:T(8,128)(2,1)S(1)}, u32[]{:S(2)}, u32[]{:S(2)}) collective-permute-start(bf16[400,128]{1,0:T(8,128)(2,1)S(1)} %get-tuple-element.33), channel_id=1, source_target_pairs={{0,3},{1,0},{2,1},{3,2},{4,7},{5,4},{6,5},{7,6},{8,11},{9,8},{10,9... | collective-permute-start | bytes 307208 | tf_op jit(solution)/shard_map/ppermute | solution.py:359
  101.3 1.5 %collective-permute-done.pieces_1_ = bf16[400,128]{1,0:T(8,128)(2,1)S(1)} collective-permute-done((bf16[400,128]{1,0:T(8,128)(2,1)S(1)}, bf16[400,128]{1,0:T(8,128)(2,1)S(1)}, u32[]{:S(2)}, u32[]{:S(2)}) %collective-permute-start) | collective-permute-done | bytes 102432 | tf_op jit(solution)/shard_map/ppermute | solution.py:359
  102.8 1.2 %collective-permute-done.1.pieces_2_ = bf16[400,128]{1,0:T(8,128)(2,1)S(1)} collective-permute-done((bf16[400,128]{1,0:T(8,128)(2,1)S(1)}, bf16[400,128]{1,0:T(8,128)(2,1)S(1)}, u32[]{:S(2)}, u32[]{:S(2)}) %collective-permute-start.1) | collective-permute-done | bytes 102432 | tf_op jit(solution)/shard_map/ppermute | solution.py:359
  104.0 6.9 %collective-permute-done.2.pieces_3_ = bf16[400,128]{1,0:T(8,128)(2,1)S(1)} collective-permute-done((bf16[400,128]{1,0:T(8,128)(2,1)S(1)}, bf16[400,128]{1,0:T(8,128)(2,1)S(1)}, u32[]{:S(2)}, u32[]{:S(2)}) %collective-permute-start.2) | collective-permute-done | bytes 102432 | tf_op jit(solution)/shard_map/ppermute | solution.py:359
  110.9 2.4 %collective-permute-start.3 = (bf16[64,24,128]{2,1,0:T(8,128)(2,1)S(1)}, bf16[64,24,128]{2,1,0:T(8,128)(2,1)S(1)}, u32[]{:S(2)}, u32[]{:S(2)}) collective-permute-start(bf16[64,24,128]{2,1,0:T(8,128)(2,1)S(1)} %all-to-all-done.3.near), channel_id=1, source_target_pairs={{0,4},{4,0},{1,5},{5,1},{2,6},{6,2},{3,7},{7,3},{8,12},{12,8},{9,1... | collective-permute-start | bytes 1179656 | tf_op jit(solution)/shard_map/ppermute | solution.py:391
  113.3 0.8 shard_map.123
  114.1 0.5 collective-permute-done.3.far
  114.6 1.2 %shard_map.124 = (bf16[80,2880]{1,0:T(8,128)(2,1)}, f32[4,2880]{1,0:T(4,128)}, f32[4,2880]{1,0:T(4,128)}, f32[4,2880]{1,0:T(4,128)}) custom-call(s32[1]{0:T(128)} %bitcast.10.core, bf16[64,24,128]{2,1,0:T(8,128)(2,1)S(1)} %all-to-all-done.3.near, bf16[64,24,128]{2,1,0:T(8,128)(2,1)S(1)} %collective-permute-done.3.far, f32[4,2880]{1,0:T(4,128)S(1)} %copy-done.3, ...), custom_call_target="tpu_custom_call" | custom-call | tf_op jit(solution)/shard_map/pallas_call | solution.py:392
  (13 shorter events, 0.1 us)
Async XLA Ops:
  14.2 12.6 %copy-start = (bf16[80,2880]{1,0:T(8,128)(2,1)S(1)}, bf16[80,2880]{1,0:T(8,128)(2,1)}, u32[]{:S(2)}) copy-start(bf16[80,2880]{1,0:T(8,128)(2,1)} %weight.1) | copy-start | bytes 1382404
  14.2 21.1 %all-to-all-start = ((bf16[4,400,128]{2,1,0:T(8,128)(2,1)}), bf16[4,400,128]{2,1,0:T(8,128)(2,1)S(1)}, u32[]{:S(2)}, u32[]{:S(2)}) async-start(bf16[4,400,128]{2,1,0:T(8,128)(2,1)} %pack.1), calls=%async_computation | async-start | bytes 819200 | tf_op jit(solution)/shard_map/all_to_all | solution.py:286
  25.2 0.7 copy-start.6
  27.2 0.8 copy-start.3
  27.2 0.8 copy-start.4
  27.2 0.8 copy-start.5
  83.6 27.3 %all-to-all-start.3 = ((bf16[64,24,128]{2,1,0:T(8,128)(2,1)}), bf16[64,24,128]{2,1,0:T(8,128)(2,1)S(1)}, u32[]{:S(2)}, u32[]{:S(2)}) async-start(bf16[64,24,128]{2,1,0:T(8,128)(2,1)} %shard_map.121), calls=%async_computation.3 | async-start | bytes 786432 | tf_op jit(solution)/shard_map/all_to_all | solution.py:286
  89.3 24.0 %copy-start.1 = (bf16[1,1,320,128]{3,2,1,0:T(8,128)(2,1)S(1)}, bf16[1,1,320,128]{3,2,1,0:T(8,128)(2,1)}, u32[]{:S(2)}) copy-start(bf16[1,1,320,128]{3,2,1,0:T(8,128)(2,1)} %param.7) | copy-start | bytes 245764
  89.3 24.0 %copy-start.2 = (bf16[1,1,320,128]{3,2,1,0:T(8,128)(2,1)S(1)}, bf16[1,1,320,128]{3,2,1,0:T(8,128)(2,1)}, u32[]{:S(2)}) copy-start(bf16[1,1,320,128]{3,2,1,0:T(8,128)(2,1)} %param.8) | copy-start | bytes 245764
  90.7 12.1 %collective-permute-start = (bf16[400,128]{1,0:T(8,128)(2,1)S(1)}, bf16[400,128]{1,0:T(8,128)(2,1)S(1)}, u32[]{:S(2)}, u32[]{:S(2)}) collective-permute-start(bf16[400,128]{1,0:T(8,128)(2,1)S(1)} %get-tuple-element.31), channel_id=1, source_target_pairs={{0,1},{1,2},{2,3},{3,0},{4,5},{5,6},{6,7},{7,4},{8,9},{9,10},{10,1... | collective-permute-start | bytes 307208 | tf_op jit(solution)/shard_map/ppermute | solution.py:359
  93.2 10.8 %collective-permute-start.1 = (bf16[400,128]{1,0:T(8,128)(2,1)S(1)}, bf16[400,128]{1,0:T(8,128)(2,1)S(1)}, u32[]{:S(2)}, u32[]{:S(2)}) collective-permute-start(bf16[400,128]{1,0:T(8,128)(2,1)S(1)} %get-tuple-element.32), channel_id=1, source_target_pairs={{0,2},{1,3},{2,0},{3,1},{4,6},{5,7},{6,4},{7,5},{8,10},{9,11},{10,... | collective-permute-start | bytes 307208 | tf_op jit(solution)/shard_map/ppermute | solution.py:359
  96.8 14.2 %collective-permute-start.2 = (bf16[400,128]{1,0:T(8,128)(2,1)S(1)}, bf16[400,128]{1,0:T(8,128)(2,1)S(1)}, u32[]{:S(2)}, u32[]{:S(2)}) collective-permute-start(bf16[400,128]{1,0:T(8,128)(2,1)S(1)} %get-tuple-element.33), channel_id=1, source_target_pairs={{0,3},{1,0},{2,1},{3,2},{4,7},{5,4},{6,5},{7,6},{8,11},{9,8},{10,9... | collective-permute-start | bytes 307208 | tf_op jit(solution)/shard_map/ppermute | solution.py:359
  110.9 3.7 %collective-permute-start.3 = (bf16[64,24,128]{2,1,0:T(8,128)(2,1)S(1)}, bf16[64,24,128]{2,1,0:T(8,128)(2,1)S(1)}, u32[]{:S(2)}, u32[]{:S(2)}) collective-permute-start(bf16[64,24,128]{2,1,0:T(8,128)(2,1)S(1)} %all-to-all-done.3.near), channel_id=1, source_target_pairs={{0,4},{4,0},{1,5},{5,1},{2,6},{6,2},{3,7},{7,3},{8,12},{12,8},{9,1... | collective-permute-start | bytes 1179656 | tf_op jit(solution)/shard_map/ppermute | solution.py:391
where the time goes:
time: 116 us
  blocking collectives  45.2 us (39%)
  starting transfers between devices  29.4 us (25%)
  Pallas kernels  20 us (17%)
  waiting for transfers between devices  16.6 us (14%)
  local copies, waits for them, and re-layouts  2.21 us (2%)
  other arithmetic  1.51 us (1%)
    all_to_all x2, blocking collectives, exchange(): return lax.all_to_all(value, axes, 0, 0, tiled=True)  45.2 us
    all_to_all x2, starting transfers between devices, exchange(): return lax.all_to_all(value, axes, 0, 0, tiled=True)  16.4 us
    pallas_call x1, Pallas kernels, local(): pl.pallas_call(pack_body, out_shape=jax.ShapeDtypeStruct((strips, channel...  13.6 us
    ppermute x3, starting transfers between devices, local(): lax.ppermute(result, 'strip', [(i, (i + ahead) % strips) for i in range(s...  10.6 us
    ppermute x3, waiting for transfers between devices, local(): lax.ppermute(result, 'strip', [(i, (i + ahead) % strips) for i in range(s...  9.65 us
    all_to_all x2, waiting for transfers between devices, exchange(): return lax.all_to_all(value, axes, 0, 0, tiled=True)  6.46 us
    ppermute x1, starting transfers between devices, local(): far = lax.ppermute(near, 'core', [(i, cores - 1 - i) for i in range(cores)])  2.39 us
  transfers between devices with their start and end apart: 6, of which 5 were waited for; matrix products, arithmetic and copies ran while one was open for 2% of the time, Pallas kernels for 2%

commit v1 on v0

v1 whole, which is shorter than its diff:
```python
import functools
import jax
import jax.numpy as jnp
from jax import lax
from jax.experimental import pallas as pl
from jax.experimental.pallas import tpu as pltpu
from jax.sharding import Mesh, PartitionSpec as P

beta_first = 0.9
beta_second = 0.999
learn_rate = 0.01
epsilon = 1e-08
bias_first = 1.0 - 0.9**10
bias_second = 1.0 - 0.999**10

interpret = False
LANES = 128
RANK_SHAPE = (8, 8, 2)
TERMS = 2
taps = [(dh, dw) for dh in (-1, 0, 1) for dw in (-1, 0, 1)]
f32 = jnp.float32
bf16 = jnp.bfloat16


def call(body, out_shape, scratch=(), scalars=0, inputs=0):
    specs = {}
    if scalars:
        specs["in_specs"] = [pl.BlockSpec(memory_space=pltpu.SMEM)] * scalars + [
            pl.BlockSpec(memory_space=pltpu.VMEM)
        ] * inputs
    return pl.pallas_call(
        body,
        out_shape=out_shape,
        scratch_shapes=scratch,
        interpret=interpret,
        compiler_params=pltpu.CompilerParams(vmem_limit_bytes=20 << 20),
        **specs,
    )


def dot(left, right, left_dim, right_dim):
    return lax.dot_general(
        left, right, (((left_dim,), (right_dim,)), ((), ())), preferred_element_type=f32
    )


def shifted(value):
    lane = lax.broadcasted_iota(jnp.int32, value.shape, 1)
    last = value.shape[1] - 1
    before = jnp.where(lane == 0, 0.0, pltpu.roll(value, 1, 1))
    after = jnp.where(lane == last, 0.0, pltpu.roll(value, last, 1))
    return {-1: before.astype(bf16), 0: value.astype(bf16), 1: after.astype(bf16)}


def fill(cols, rows, load, direction):
    first = load(0)
    count, width = first.shape
    for index, (dh, _) in enumerate(taps):
        for h in range(rows):
            if not 0 <= h + direction * dh < rows:
                cols[index * count : (index + 1) * count, h * width : (h + 1) * width] = jnp.zeros(
                    (count, width), bf16
                )
    for source in range(rows):
        versions = shifted(first if source == 0 else load(source))
        for index, (dh, dw) in enumerate(taps):
            h = source - direction * dh
            if 0 <= h < rows:
                cols[index * count : (index + 1) * count, h * width : (h + 1) * width] = versions[
                    direction * dw
                ]


def activated(gathered, channels, h):
    value = gathered[h, :channels, :].astype(f32)
    return (value / (1.0 + jnp.exp(-value))).astype(bf16).astype(f32)


def pack_body(pixels, upstream, outgoing, staged, arrived):
    strips, channels = outgoing.shape[0], pixels.shape[0]
    loads = [
        pltpu.make_async_copy(pixels, staged.at[:channels, :], arrived.at[0]),
        pltpu.make_async_copy(upstream, staged.at[channels:, :], arrived.at[1]),
    ]
    for load in loads:
        load.start()
    for load in loads:
        load.wait()
    quarter = channels // strips
    for strip in range(strips):
        outgoing[strip, :channels, :] = staged[:channels, :]
        outgoing[strip, channels:, :] = staged[
            channels + strip * quarter : channels + (strip + 1) * quarter, :
        ]


def split_body(master, first_moment, second_moment, pieces, *, step):
    state = jnp.concatenate([master[...], first_moment[...], second_moment[...]], axis=0)
    terms = []
    for _ in range(TERMS):
        term = state.astype(bf16).astype(f32)
        terms.append(term)
        state = state - term
    terms = jnp.concatenate(terms, axis=0)
    halves, height, padded = pieces.shape
    excess = (halves - 1) * step + padded - terms.shape[1]
    terms = jnp.concatenate([terms, jnp.zeros((height, excess), f32)], axis=1)
    for half in range(halves):
        pieces[half] = terms[:, half * step : half * step + padded].astype(bf16)


def gradient_body(core, gathered, pieces, kept, sent, cols, *, channels, step):
    rows = gathered.shape[0]
    quarter = gathered.shape[1] - channels
    fill(cols, rows, functools.partial(activated, gathered, channels), 1)
    whole = len(taps) * channels
    if cols.shape[0] > whole:
        cols[whole:, :] = jnp.zeros((cols.shape[0] - whole, cols.shape[1]), bf16)
    upstream = jnp.concatenate([gathered[h, channels:, :] for h in range(rows)], axis=1)
    padded = kept.shape[1]
    for target, half in ((sent, 1 - core[0]), (kept, core[0])):
        start = pl.multiple_of(half * step, 8)
        product = dot(upstream, cols[pl.ds(start, padded), :], 1, 1)
        target[:quarter, :] = product.astype(bf16)
        target[quarter:, :] = pieces[half]


def convolution_body(
    strip, gathered, residual, weight, turned, *results, channels
):
    *results, cols, back_cols, whole = results
    rows, quarter, width = residual.shape
    fill(cols, rows, functools.partial(activated, gathered, channels), 1)
    convolved = dot(weight[...], cols[...], 1, 0)
    for h in range(rows):
        whole[h, :quarter, :] = (
            residual[h].astype(f32) + convolved[:, h * width : (h + 1) * width]
        ).astype(bf16)
    fill(back_cols, rows, lambda h: gathered[h, channels:, :].astype(f32), -1)
    spread = dot(turned[...], back_cols[...], 1, 0)
    for h in range(rows):
        whole[h, quarter:, :] = spread[:, h * width : (h + 1) * width].astype(bf16)
    for ahead, result in enumerate(results):
        target = strip[0] + ahead
        result[...] = whole[jnp.where(target >= rows, target - rows, target)]


def collect_body(strip, pixels, upstream, *pieces, quarter):
    *pieces, output, grad_input = pieces
    strips = len(pieces)
    spread = jnp.zeros(pixels.shape, f32)
    for behind, piece in enumerate(pieces):
        source = strip[0] - behind
        source = jnp.where(source < 0, source + strips, source)
        output[pl.ds(pl.multiple_of(source * quarter, quarter), quarter), :] = piece[:quarter, :]
        spread = spread + piece[quarter:, :].astype(f32)
    value = pixels[...].astype(f32)
    sigmoid = 1.0 / (1.0 + jnp.exp(-value))
    derivative = sigmoid * (1.0 + value * (1.0 - sigmoid))
    grad_input[...] = (upstream[...].astype(f32) + spread * derivative).astype(bf16)


def turn_body(core, kept, received, message, *, quarter):
    ours, others = kept[...].astype(f32), received[...].astype(f32)
    first = core[0] == 0
    rows = [
        ours[:quarter] + others[:quarter],
        jnp.where(first, ours[quarter:], others[quarter:]),
        jnp.where(first, others[quarter:], ours[quarter:]),
    ]
    spare = LANES - 2 * ours.shape[0] + quarter
    if spare:
        rows.append(jnp.zeros((spare, ours.shape[1]), f32))
    turned = jnp.transpose(jnp.concatenate(rows, axis=0))
    chips, chunk, _ = message.shape
    for chip in range(chips):
        message[chip] = turned[chip * chunk : (chip + 1) * chunk, :].astype(bf16)


def adam(grads, master, first_moment, second_moment):
    first_new = beta_first * first_moment + (1.0 - beta_first) * grads
    second_new = beta_second * second_moment + (1.0 - beta_second) * grads * grads
    update = learn_rate * (first_new / bias_first) / (jnp.sqrt(second_new / bias_second) + epsilon)
    return master - update, first_new, second_new


def publish_body(strip, received, slots, message, *, quarter, capacity, cores, root):
    chips, chunk, _ = received.shape
    strips = slots.shape[0]
    columns = max(LANES, chips * cores * capacity)
    mine = slots[0:1, :]
    for other in range(1, strips):
        mine = jnp.where(strip[0] == other, slots[other : other + 1, :], mine)
    wide = jnp.concatenate([mine] * 3, axis=1)
    owner, place = wide // capacity, wide % capacity
    share = TERMS * 3 * capacity
    row = lax.broadcasted_iota(jnp.int32, (LANES, 3 * LANES), 0) - quarter
    array = lax.broadcasted_iota(jnp.int32, (LANES, 3 * LANES), 1) // LANES
    within = row % (3 * capacity)
    here = (row >= 0) & (row < cores * share) & (wide >= 0) & (row // share == owner % cores)
    here = here & (within // capacity == array) & (within % capacity == place)
    here = jnp.where(here, 1.0, 0.0).astype(bf16)
    values = [received[chip].astype(f32) for chip in range(chips)]
    grads = values[0]
    for value in values[1:]:
        grads = grads + value
    picked = dot(jnp.concatenate(values, axis=0).astype(bf16), here, 1, 0)
    state = jnp.zeros((chunk, 3 * LANES), f32)
    for chip in range(chips):
        state = jnp.where(
            owner // cores == chip, picked[chip * chunk : (chip + 1) * chunk], state
        )
    fresh, _, _ = adam(
        grads / root, state[:, :LANES], state[:, LANES : 2 * LANES], state[:, 2 * LANES :]
    )
    index = lax.broadcasted_iota(jnp.int32, (columns, LANES), 0)
    matches = jnp.where(index == mine, 1.0, 0.0).astype(bf16)
    chosen = dot(grads.astype(bf16), matches, 1, 1)
    lane = lax.broadcasted_iota(jnp.int32, (chunk, LANES), 1)
    span = cores * capacity
    per_tile = LANES // span
    for chip in range(chips):
        tile = chosen[:, chip // per_tile * LANES : (chip // per_tile + 1) * LANES]
        shift = (quarter - span * (chip % per_tile)) % LANES
        moved = tile if shift == 0 else pltpu.roll(tile, shift, 1)
        value = jnp.where(lane < quarter, fresh, jnp.where(lane < quarter + span, moved, 0.0))
        message[chip] = value.astype(bf16)


def flat(messages):
    chips, chunk, _ = messages.shape
    return messages[...].astype(f32).reshape(chips * chunk, LANES)


def unit(rows, first):
    shape = (rows, LANES)
    row = lax.broadcasted_iota(jnp.int32, shape, 0)
    return jnp.where(row + first == lax.broadcasted_iota(jnp.int32, shape, 1), 1.0, 0.0).astype(
        bf16
    )


def owned_body(near, message, *, quarter, capacity, strips):
    targets, height, _ = message.shape
    turned = dot(unit(16, quarter), flat(near).astype(bf16), 1, 1)
    for target in range(targets):
        first = target // strips * capacity
        rows = turned[first : first + capacity]
        rows = jnp.concatenate([rows, jnp.zeros((height - capacity, rows.shape[1]), f32)], axis=0)
        message[target] = rows.astype(bf16)


def finish_body(
    core, near, far, owned, master, first_moment, second_moment, filled,
    new_weight, new_master, new_first, new_second, *, step, strips, root,
):
    quarter, capacity = new_weight.shape[0], master.shape[0]
    ours, others = flat(near), flat(far)
    first = core[0] == 0
    rows = [jnp.where(first, ours, others)[:step], jnp.where(first, others, ours)[:step]]
    rows = jnp.concatenate(rows, axis=0).astype(bf16)
    turned = dot(unit(quarter, 0), rows, 1, 1)
    new_weight[...] = turned.astype(bf16)
    halves = []
    for half in range(owned.shape[0] // strips):
        total = owned[half * strips].astype(f32)
        for strip in range(1, strips):
            total = total + owned[half * strips + strip].astype(f32)
        halves.append(total[:capacity, :step])
    grads = jnp.concatenate(halves, axis=1) / root
    fresh, first_new, second_new = adam(
        grads, master[...], first_moment[...], second_moment[...]
    )
    keep = filled[...] > 0.0
    new_master[...] = jnp.where(keep, fresh, master[...])
    new_first[...] = jnp.where(keep, first_new, first_moment[...])
    new_second[...] = jnp.where(keep, second_new, second_moment[...])


def slot_tables(owner_list, capacity):
    count = owner_list.shape[0]
    same_owner = owner_list[:, None] == owner_list[None, :]
    order = jnp.arange(count, dtype=jnp.int32)
    earlier = order[None, :] < order[:, None]
    return owner_list * capacity + jnp.sum((same_owner & earlier).astype(jnp.int32), axis=1)


def exchange(value, axes):
    return lax.all_to_all(value, axes, 0, 0, tiled=True)


def local(latents, cotangent, weight, master, first_moment, second_moment, owner_list):
    lines, groups, cores, strips = (lax.axis_size(a) for a in ("line", "group", "core", "strip"))
    chips = lines * groups
    ranks = chips * cores
    strip, core = lax.axis_index("strip"), lax.axis_index("core")
    rank = (lax.axis_index("line") * groups + lax.axis_index("group")) * cores + core
    strip_scalar = strip.reshape(1).astype(jnp.int32)
    core_scalar = core.reshape(1).astype(jnp.int32)
    swap = [(i, cores - 1 - i) for i in range(cores)]
    channels, width = latents.shape[2:]
    quarter = channels // strips
    capacity = master.shape[0]
    height = TERMS * 3 * capacity
    taken = len(taps) * channels
    step = taken // cores
    padded = -(-step // LANES) * LANES
    chunk = padded // chips
    rows = strips
    root = float(ranks * rows * width) ** 0.5
    pixels, upstream = latents[0, 0], cotangent[0, 0]

    outgoing = pl.pallas_call(
        pack_body,
        out_shape=jax.ShapeDtypeStruct((strips, channels + quarter, width), bf16),
        in_specs=[pl.BlockSpec(memory_space=pltpu.HBM)] * 2,
        scratch_shapes=[
            pltpu.VMEM((2 * channels, width), bf16),
            pltpu.SemaphoreType.DMA((2,)),
        ],
        name="pack",
        interpret=interpret,
        compiler_params=pltpu.CompilerParams(vmem_limit_bytes=4 << 20),
    )(pixels, upstream)
    gathered = exchange(outgoing, "strip")

    slot_ids = slot_tables(owner_list, capacity)
    slots = jnp.pad(
        slot_ids.reshape(strips, quarter), ((0, 0), (0, LANES - quarter)), constant_values=-1
    )
    owned = jnp.sum((owner_list == rank).astype(jnp.int32))
    filled = (jnp.arange(capacity, dtype=jnp.int32) < owned).astype(f32)[:, None]
    turned = weight.reshape(quarter, len(taps), channels).transpose(2, 1, 0)
    turned = turned.reshape(channels, len(taps) * quarter)
    pieces = call(
        functools.partial(split_body, step=step),
        jax.ShapeDtypeStruct((cores, height, padded), bf16),
    )(master, first_moment, second_moment)
    gathered, slots, filled, turned, pieces = lax.optimization_barrier(
        (gathered, slots, filled, turned, pieces)
    )

    kept, sent = call(
        functools.partial(gradient_body, channels=channels, step=step),
        [jax.ShapeDtypeStruct((quarter + height, padded), bf16)] * 2,
        [pltpu.VMEM(((cores - 1) * step + padded, rows * width), bf16)],
        scalars=1,
        inputs=2,
    )(core_scalar, gathered, pieces)
    swapped = lax.ppermute(sent, "core", swap)

    residual = lax.dynamic_slice_in_dim(gathered, strip * quarter, quarter, axis=1)
    results = call(
        functools.partial(convolution_body, channels=channels),
        [jax.ShapeDtypeStruct((quarter + channels, width), bf16)] * strips,
        [
            pltpu.VMEM((taken, rows * width), bf16),
            pltpu.VMEM((len(taps) * quarter, rows * width), bf16),
            pltpu.VMEM((rows, quarter + channels, width), bf16),
        ],
        scalars=1,
        inputs=4,
    )(strip_scalar, gathered, residual, weight, turned)

    returned = [
        lax.ppermute(result, "strip", [(i, (i + ahead) % strips) for i in range(strips)])
        if ahead
        else result
        for ahead, result in enumerate(results)
    ]

    by_chip = call(
        functools.partial(turn_body, quarter=quarter),
        jax.ShapeDtypeStruct((chips, chunk, LANES), bf16),
        scalars=1,
        inputs=2,
    )(core_scalar, kept, swapped)
    by_chip = exchange(by_chip, ("line", "group"))
    message = call(
        functools.partial(publish_body, quarter=quarter, capacity=capacity, cores=cores, root=root),
        jax.ShapeDtypeStruct((chips, chunk, LANES), bf16),
        scalars=1,
        inputs=2,
    )(strip_scalar, by_chip, slots)
    near = exchange(message, ("line", "group"))

    near, *returned = lax.optimization_barrier((near, *returned))
    output, grad_input = call(
        functools.partial(collect_body, quarter=quarter),
        [jax.ShapeDtypeStruct((channels, width), bf16)] * 2,
        scalars=1,
        inputs=2 + strips,
    )(strip_scalar, pixels, upstream, *returned)

    far = lax.ppermute(near, "core", swap)
    owned_rows = call(
        functools.partial(owned_body, quarter=quarter, capacity=capacity, strips=strips),
        jax.ShapeDtypeStruct((cores * strips, 8, padded), bf16),
    )(near)
    owned_rows = exchange(owned_rows, ("core", "strip"))
    new_weight, new_master, new_first, new_second = call(
        functools.partial(finish_body, step=step, strips=strips, root=root),
        [jax.ShapeDtypeStruct((quarter, taken), bf16)]
        + [jax.ShapeDtypeStruct(master.shape, f32)] * 3,
        scalars=1,
        inputs=7,
    )(core_scalar, near, far, owned_rows, master, first_moment, second_moment, filled)
    return (output[None, None], grad_input[None, None], new_weight, new_master, new_first, new_second)


def solution(mesh):
    fine = Mesh(
        mesh.devices.reshape(RANK_SHAPE + (mesh.shape["strip"],)),
        ("line", "group", "core", "strip"),
    )
    ranks = ("line", "group", "core")
    images = P(ranks, "strip", None, None)
    specs = (images, images, P("strip", None), P(ranks, None), P(ranks, None), P(ranks, None))

    return jax.shard_map(
        local, mesh=fine, in_specs=specs + (P(),), out_specs=specs, check_vma=False
    )
```

time: 116 us -> 108 us (0.931)
  blocking collectives: 45.2 us -> 0 us
  starting transfers between devices: 29.4 us -> 53.2 us
  waiting for transfers between devices: 16.6 us -> 38.4 us
  Pallas kernels: 20 us -> 9.12 us
  local copies, waits for them, and re-layouts: 2.21 us -> 4.02 us
    all_to_all x2 -> x0, blocking collectives: 45.2 us -> none  [exchange(): return lax.all_to_all(value, axes, 0, 0, tiled=True)]
    all_to_all x2 -> x4, waiting for transfers between devices: 6.46 us -> 27.9 us  [exchange(): return lax.all_to_all(value, axes, 0, 0, tiled=True)]
    all_to_all x2 -> x4, starting transfers between devices: 16.4 us -> 33.5 us  [exchange(): return lax.all_to_all(value, axes, 0, 0, tiled=True)]
    pallas_call x1, Pallas kernels: 13.6 us -> 1 us  [local(): pl.pallas_call(pack_body, out_shape=jax.ShapeDtypeStruct((strips, channel...]
    ppermute x1 -> x2, starting transfers between devices: 2.39 us -> 8.76 us  [the longest x1 6.29 us: local(): swapped = lax.ppermute(sent, 'core', swap)]
    unnamed x15 -> x19, local copies, waits for them, and re-layouts: 1.5 us -> 3.32 us
    pallas_call x4 -> x5, Pallas kernels: 2.85 us -> 4.66 us  [the longest x1 1.54 us: local(): call(functools.partial(gradient_body, channels=channels, step=step), [jax...]
  transfers between devices with their start and end apart: 6 -> 9, of which waited for: 5 -> 7; matrix products, arithmetic and copies ran while one was open for 2% -> 2% of each run, Pallas kernels for 2% -> 3%
where the time goes in v1:
time: 108 us; the launch traced here: 107 us
  starting transfers between devices  53.2 us (49%)
  waiting for transfers between devices  38.4 us (36%)
  Pallas kernels  9.12 us (8%)
  local copies, waits for them, and re-layouts  4.02 us (4%)
  other arithmetic  1.51 us (1%)
    all_to_all x4, starting transfers between devices, exchange(): return lax.all_to_all(value, axes, 0, 0, tiled=True)  33.5 us
    all_to_all x4, waiting for transfers between devices, exchange(): return lax.all_to_all(value, axes, 0, 0, tiled=True)  27.9 us
    ppermute x3, starting transfers between devices, local(): lax.ppermute(result, 'strip', [(i, (i + ahead) % strips) for i in range(s...  10.9 us
    ppermute x3, waiting for transfers between devices, local(): lax.ppermute(result, 'strip', [(i, (i + ahead) % strips) for i in range(s...  9.25 us
    ppermute x1, starting transfers between devices, local(): swapped = lax.ppermute(sent, 'core', swap)  6.29 us
    unnamed x19, local copies, waits for them, and re-layouts  3.32 us
    ppermute x1, starting transfers between devices, local(): far = lax.ppermute(near, 'core', swap)  2.47 us
  transfers between devices with their start and end apart: 9, of which 7 were waited for; matrix products, arithmetic and copies ran while one was open for 2% of the time, Pallas kernels for 3%

profile of v1, /device:TPU:1, one launch (start us, length us, event | category | flops | bytes accessed | tf_op | source)
XLA Modules:
  0.0 107.1 jit_solution(16763098566401843357)
XLA Ops:
  0.6 0.9 copy-done.1
  1.5 0.9 copy-done.3
  2.4 1.0 pack.1
  3.4 11.0 %all-to-all-start = ((bf16[4,400,128]{2,1,0:T(8,128)(2,1)}), bf16[4,400,128]{2,1,0:T(8,128)(2,1)S(1)}, u32[]{:S(2)}, u32[]{:S(2)}) async-start(bf16[4,400,128]{2,1,0:T(8,128)(2,1)} %pack.1), calls=%async_computation | async-start | bytes 819200 | tf_op jit(solution)/shard_map/all_to_all | solution.py:289
  14.4 0.7 copy-done.8
  15.3 0.6 convert_reduce_fusion.1
  16.0 0.4 copy.17
  16.5 0.4 copy.18
  16.8 0.4 copy-done.5
  17.4 0.7 fusion.1.filled
  18.1 6.5 %all-to-all-done.gathered = bf16[4,400,128]{2,1,0:T(8,128)(2,1)S(1)} async-done(((bf16[4,400,128]{2,1,0:T(8,128)(2,1)}), bf16[4,400,128]{2,1,0:T(8,128)(2,1)S(1)}, u32[]{:S(2)}, u32[]{:S(2)}) %all-to-all-start) | async-done | bytes 409632 | tf_op jit(solution)/shard_map/all_to_all | solution.py:289
  24.5 1.5 %shard_map.119 = (bf16[104,1536]{1,0:T(8,128)(2,1)S(1)}, bf16[104,1536]{1,0:T(8,128)(2,1)S(1)}) custom-call(s32[1]{0:T(128)} %bitcast.3.core, bf16[4,400,128]{2,1,0:T(8,128)(2,1)S(1)} %all-to-all-done.gathered, bf16[2,24,1536]{2,1,0:T(8,128)(2,1)S(1)} %shard_map.118.pieces), custom_call_target="tpu_custom_call" | custom-call | tf_op jit(solution)/shard_map/pallas_call | solution.py:343
  26.1 6.3 %collective-permute-start = (bf16[104,1536]{1,0:T(8,128)(2,1)S(1)}, bf16[104,1536]{1,0:T(8,128)(2,1)S(1)}, u32[]{:S(2)}, u32[]{:S(2)}) collective-permute-start(bf16[104,1536]{1,0:T(8,128)(2,1)S(1)} %get-tuple-element.31), channel_id=1, source_target_pairs={{0,4},{4,0},{1,5},{5,1},{2,6},{6,2},{3,7},{7,3},{8,12},{12,8},{9,1... | collective-permute-start | bytes 958472 | tf_op jit(solution)/shard_map/ppermute | solution.py:350
  32.4 1.2 %collective-permute-done.received = bf16[104,1536]{1,0:T(8,128)(2,1)S(1)} collective-permute-done((bf16[104,1536]{1,0:T(8,128)(2,1)S(1)}, bf16[104,1536]{1,0:T(8,128)(2,1)S(1)}, u32[]{:S(2)}, u32[]{:S(2)}) %collective-permute-start) | collective-permute-done | bytes 319520 | tf_op jit(solution)/shard_map/ppermute | solution.py:350
  33.6 0.9 shard_map.120
  34.5 11.4 %all-to-all-start.1 = ((bf16[64,24,128]{2,1,0:T(8,128)(2,1)}), bf16[64,24,128]{2,1,0:T(8,128)(2,1)S(1)}, u32[]{:S(2)}, u32[]{:S(2)}) async-start(bf16[64,24,128]{2,1,0:T(8,128)(2,1)} %shard_map.120), calls=%async_computation.1 | async-start | bytes 786432 | tf_op jit(solution)/shard_map/all_to_all | solution.py:289
  45.9 13.2 %all-to-all-done.1.received = bf16[64,24,128]{2,1,0:T(8,128)(2,1)S(1)} async-done(((bf16[64,24,128]{2,1,0:T(8,128)(2,1)}), bf16[64,24,128]{2,1,0:T(8,128)(2,1)S(1)}, u32[]{:S(2)}, u32[]{:S(2)}) %all-to-all-start.1) | async-done | bytes 393248 | tf_op jit(solution)/shard_map/all_to_all | solution.py:289
  59.1 1.4 %shard_map.121 = bf16[64,24,128]{2,1,0:T(8,128)(2,1)} custom-call(s32[1]{0:T(128)} %bitcast.strip, bf16[64,24,128]{2,1,0:T(8,128)(2,1)S(1)} %all-to-all-done.1.received, s32[4,128]{1,0:T(4,128)S(1)} %pad.4.slots), custom_call_target="tpu_custom_call" | custom-call | tf_op jit(solution)/shard_map/pallas_call | solution.py:379
  60.5 6.9 %all-to-all-start.2 = ((bf16[64,24,128]{2,1,0:T(8,128)(2,1)}), bf16[64,24,128]{2,1,0:T(8,128)(2,1)S(1)}, u32[]{:S(2)}, u32[]{:S(2)}) async-start(bf16[64,24,128]{2,1,0:T(8,128)(2,1)} %shard_map.121), calls=%async_computation.2 | async-start | bytes 786432 | tf_op jit(solution)/shard_map/all_to_all | solution.py:289
  67.7 1.3 %shard_map.122 = (bf16[400,128]{1,0:T(8,128)(2,1)S(1)}, bf16[400,128]{1,0:T(8,128)(2,1)S(1)}, bf16[400,128]{1,0:T(8,128)(2,1)S(1)}, bf16[400,128]{1,0:T(8,128)(2,1)S(1)}) custom-call(s32[1]{0:T(128)} %bitcast.strip, bf16[4,400,128]{2,1,0:T(8,128)(2,1)S(1)} %all-to-all-done.gathered, bf16[4,80,128]{2,1,0:T(8,128)(2,1)S(1)} %constant_dynamic-slice_fusion.residual, ...), custom_call_target="tpu_custom_call" | custom-call | tf_op jit(solution)/shard_map/pallas_call | solution.py:353
  69.1 2.6 %collective-permute-start.1 = (bf16[400,128]{1,0:T(8,128)(2,1)S(1)}, bf16[400,128]{1,0:T(8,128)(2,1)S(1)}, u32[]{:S(2)}, u32[]{:S(2)}) collective-permute-start(bf16[400,128]{1,0:T(8,128)(2,1)S(1)} %get-tuple-element.35), channel_id=1, source_target_pairs={{0,1},{1,2},{2,3},{3,0},{4,5},{5,6},{6,7},{7,4},{8,9},{9,10},{10,1... | collective-permute-start | bytes 307208 | tf_op jit(solution)/shard_map/ppermute | solution.py:366
  71.7 4.9 %collective-permute-start.2 = (bf16[400,128]{1,0:T(8,128)(2,1)S(1)}, bf16[400,128]{1,0:T(8,128)(2,1)S(1)}, u32[]{:S(2)}, u32[]{:S(2)}) collective-permute-start(bf16[400,128]{1,0:T(8,128)(2,1)S(1)} %get-tuple-element.36), channel_id=1, source_target_pairs={{0,2},{1,3},{2,0},{3,1},{4,6},{5,7},{6,4},{7,5},{8,10},{9,11},{10,... | collective-permute-start | bytes 307208 | tf_op jit(solution)/shard_map/ppermute | solution.py:366
  76.5 3.4 %collective-permute-start.3 = (bf16[400,128]{1,0:T(8,128)(2,1)S(1)}, bf16[400,128]{1,0:T(8,128)(2,1)S(1)}, u32[]{:S(2)}, u32[]{:S(2)}) collective-permute-start(bf16[400,128]{1,0:T(8,128)(2,1)S(1)} %get-tuple-element.37), channel_id=1, source_target_pairs={{0,3},{1,0},{2,1},{3,2},{4,7},{5,4},{6,5},{7,6},{8,11},{9,8},{10,9... | collective-permute-start | bytes 307208 | tf_op jit(solution)/shard_map/ppermute | solution.py:366
  80.0 2.5 %collective-permute-done.1.pieces_1_ = bf16[400,128]{1,0:T(8,128)(2,1)S(1)} collective-permute-done((bf16[400,128]{1,0:T(8,128)(2,1)S(1)}, bf16[400,128]{1,0:T(8,128)(2,1)S(1)}, u32[]{:S(2)}, u32[]{:S(2)}) %collective-permute-start.1) | collective-permute-done | bytes 102432 | tf_op jit(solution)/shard_map/ppermute | solution.py:366
  82.5 1.9 %collective-permute-done.2.pieces_2_ = bf16[400,128]{1,0:T(8,128)(2,1)S(1)} collective-permute-done((bf16[400,128]{1,0:T(8,128)(2,1)S(1)}, bf16[400,128]{1,0:T(8,128)(2,1)S(1)}, u32[]{:S(2)}, u32[]{:S(2)}) %collective-permute-start.2) | collective-permute-done | bytes 102432 | tf_op jit(solution)/shard_map/ppermute | solution.py:366
  84.4 4.8 %collective-permute-done.3.pieces_3_ = bf16[400,128]{1,0:T(8,128)(2,1)S(1)} collective-permute-done((bf16[400,128]{1,0:T(8,128)(2,1)S(1)}, bf16[400,128]{1,0:T(8,128)(2,1)S(1)}, u32[]{:S(2)}, u32[]{:S(2)}) %collective-permute-start.3) | collective-permute-done | bytes 102432 | tf_op jit(solution)/shard_map/ppermute | solution.py:366
  89.2 2.5 %collective-permute-start.4 = (bf16[64,24,128]{2,1,0:T(8,128)(2,1)S(1)}, bf16[64,24,128]{2,1,0:T(8,128)(2,1)S(1)}, u32[]{:S(2)}, u32[]{:S(2)}) collective-permute-start(bf16[64,24,128]{2,1,0:T(8,128)(2,1)S(1)} %all-to-all-done.2.near), channel_id=1, source_target_pairs={{0,4},{4,0},{1,5},{5,1},{2,6},{6,2},{3,7},{7,3},{8,12},{12,8},{9,1... | collective-permute-start | bytes 1179656 | tf_op jit(solution)/shard_map/ppermute | solution.py:395
  91.7 0.9 shard_map.124
  92.6 4.2 %all-to-all-start.3 = ((bf16[8,8,1536]{2,1,0:T(8,128)(2,1)}), bf16[8,8,1536]{2,1,0:T(8,128)(2,1)S(1)}, u32[]{:S(2)}, u32[]{:S(2)}) async-start(bf16[8,8,1536]{2,1,0:T(8,128)(2,1)} %shard_map.124), calls=%async_computation.3 | async-start | bytes 393216 | tf_op jit(solution)/shard_map/all_to_all | solution.py:289
  96.8 0.8 shard_map.123
  97.6 8.3 %all-to-all-done.3.owned = bf16[8,8,1536]{2,1,0:T(8,128)(2,1)S(1)} async-done(((bf16[8,8,1536]{2,1,0:T(8,128)(2,1)}), bf16[8,8,1536]{2,1,0:T(8,128)(2,1)S(1)}, u32[]{:S(2)}, u32[]{:S(2)}) %all-to-all-start.3) | async-done | bytes 196640 | tf_op jit(solution)/shard_map/all_to_all | solution.py:289
  105.9 1.2 %shard_map.125 = (bf16[80,2880]{1,0:T(8,128)(2,1)}, f32[4,2880]{1,0:T(4,128)}, f32[4,2880]{1,0:T(4,128)}, f32[4,2880]{1,0:T(4,128)}) custom-call(s32[1]{0:T(128)} %bitcast.3.core, bf16[64,24,128]{2,1,0:T(8,128)(2,1)S(1)} %all-to-all-done.2.near, bf16[64,24,128]{2,1,0:T(8,128)(2,1)S(1)} %collective-permute-done.4.far, ...), custom_call_target="tpu_custom_call" | custom-call | tf_op jit(solution)/shard_map/pallas_call | solution.py:401
  (22 shorter events, 0.8 us)
Async XLA Ops:
  0.6 0.9 copy-start.1
  1.5 0.9 copy-start.3
  3.4 12.6 %copy-start = (bf16[80,2880]{1,0:T(8,128)(2,1)S(1)}, bf16[80,2880]{1,0:T(8,128)(2,1)}, u32[]{:S(2)}) copy-start(bf16[80,2880]{1,0:T(8,128)(2,1)} %weight.1) | copy-start | bytes 1382404
  3.4 21.1 %all-to-all-start = ((bf16[4,400,128]{2,1,0:T(8,128)(2,1)}), bf16[4,400,128]{2,1,0:T(8,128)(2,1)S(1)}, u32[]{:S(2)}, u32[]{:S(2)}) async-start(bf16[4,400,128]{2,1,0:T(8,128)(2,1)} %pack.1), calls=%async_computation | async-start | bytes 819200 | tf_op jit(solution)/shard_map/all_to_all | solution.py:289
  14.4 0.7 copy-start.8
  16.4 0.8 copy-start.5
  16.5 0.8 copy-start.6
  16.5 0.8 copy-start.7
  26.1 7.5 %collective-permute-start = (bf16[104,1536]{1,0:T(8,128)(2,1)S(1)}, bf16[104,1536]{1,0:T(8,128)(2,1)S(1)}, u32[]{:S(2)}, u32[]{:S(2)}) collective-permute-start(bf16[104,1536]{1,0:T(8,128)(2,1)S(1)} %get-tuple-element.31), channel_id=1, source_target_pairs={{0,4},{4,0},{1,5},{5,1},{2,6},{6,2},{3,7},{7,3},{8,12},{12,8},{9,1... | collective-permute-start | bytes 958472 | tf_op jit(solution)/shard_map/ppermute | solution.py:350
  34.5 24.6 %all-to-all-start.1 = ((bf16[64,24,128]{2,1,0:T(8,128)(2,1)}), bf16[64,24,128]{2,1,0:T(8,128)(2,1)S(1)}, u32[]{:S(2)}, u32[]{:S(2)}) async-start(bf16[64,24,128]{2,1,0:T(8,128)(2,1)} %shard_map.120), calls=%async_computation.1 | async-start | bytes 786432 | tf_op jit(solution)/shard_map/all_to_all | solution.py:289
  60.5 28.7 %all-to-all-start.2 = ((bf16[64,24,128]{2,1,0:T(8,128)(2,1)}), bf16[64,24,128]{2,1,0:T(8,128)(2,1)S(1)}, u32[]{:S(2)}, u32[]{:S(2)}) async-start(bf16[64,24,128]{2,1,0:T(8,128)(2,1)} %shard_map.121), calls=%async_computation.2 | async-start | bytes 786432 | tf_op jit(solution)/shard_map/all_to_all | solution.py:289
  69.1 13.4 %collective-permute-start.1 = (bf16[400,128]{1,0:T(8,128)(2,1)S(1)}, bf16[400,128]{1,0:T(8,128)(2,1)S(1)}, u32[]{:S(2)}, u32[]{:S(2)}) collective-permute-start(bf16[400,128]{1,0:T(8,128)(2,1)S(1)} %get-tuple-element.35), channel_id=1, source_target_pairs={{0,1},{1,2},{2,3},{3,0},{4,5},{5,6},{6,7},{7,4},{8,9},{9,10},{10,1... | collective-permute-start | bytes 307208 | tf_op jit(solution)/shard_map/ppermute | solution.py:366
  71.7 12.7 %collective-permute-start.2 = (bf16[400,128]{1,0:T(8,128)(2,1)S(1)}, bf16[400,128]{1,0:T(8,128)(2,1)S(1)}, u32[]{:S(2)}, u32[]{:S(2)}) collective-permute-start(bf16[400,128]{1,0:T(8,128)(2,1)S(1)} %get-tuple-element.36), channel_id=1, source_target_pairs={{0,2},{1,3},{2,0},{3,1},{4,6},{5,7},{6,4},{7,5},{8,10},{9,11},{10,... | collective-permute-start | bytes 307208 | tf_op jit(solution)/shard_map/ppermute | solution.py:366
  76.5 12.7 %collective-permute-start.3 = (bf16[400,128]{1,0:T(8,128)(2,1)S(1)}, bf16[400,128]{1,0:T(8,128)(2,1)S(1)}, u32[]{:S(2)}, u32[]{:S(2)}) collective-permute-start(bf16[400,128]{1,0:T(8,128)(2,1)S(1)} %get-tuple-element.37), channel_id=1, source_target_pairs={{0,3},{1,0},{2,1},{3,2},{4,7},{5,4},{6,5},{7,6},{8,11},{9,8},{10,9... | collective-permute-start | bytes 307208 | tf_op jit(solution)/shard_map/ppermute | solution.py:366
  89.2 16.7 %collective-permute-start.4 = (bf16[64,24,128]{2,1,0:T(8,128)(2,1)S(1)}, bf16[64,24,128]{2,1,0:T(8,128)(2,1)S(1)}, u32[]{:S(2)}, u32[]{:S(2)}) collective-permute-start(bf16[64,24,128]{2,1,0:T(8,128)(2,1)S(1)} %all-to-all-done.2.near), channel_id=1, source_target_pairs={{0,4},{4,0},{1,5},{5,1},{2,6},{6,2},{3,7},{7,3},{8,12},{12,8},{9,1... | collective-permute-start | bytes 1179656 | tf_op jit(solution)/shard_map/ppermute | solution.py:395
  92.6 4.2 %copy-start.2 = (bf16[1,1,320,128]{3,2,1,0:T(8,128)(2,1)S(1)}, bf16[1,1,320,128]{3,2,1,0:T(8,128)(2,1)}, u32[]{:S(2)}) copy-start(bf16[1,1,320,128]{3,2,1,0:T(8,128)(2,1)} %param.7) | copy-start | bytes 245764
  92.6 4.2 %copy-start.4 = (bf16[1,1,320,128]{3,2,1,0:T(8,128)(2,1)S(1)}, bf16[1,1,320,128]{3,2,1,0:T(8,128)(2,1)}, u32[]{:S(2)}) copy-start(bf16[1,1,320,128]{3,2,1,0:T(8,128)(2,1)} %param.8) | copy-start | bytes 245764
  92.6 13.3 %all-to-all-start.3 = ((bf16[8,8,1536]{2,1,0:T(8,128)(2,1)}), bf16[8,8,1536]{2,1,0:T(8,128)(2,1)S(1)}, u32[]{:S(2)}, u32[]{:S(2)}) async-start(bf16[8,8,1536]{2,1,0:T(8,128)(2,1)} %shard_map.124), calls=%async_computation.3 | async-start | bytes 393216 | tf_op jit(solution)/shard_map/all_to_all | solution.py:289

commit v2 on v1

--- a/solution.py
+++ b/solution.py
@@ -241,13 +241,11 @@
 
 
 def owned_body(near, message, *, quarter, capacity, strips):
-    targets, height, _ = message.shape
+    targets = message.shape[0]
     turned = dot(unit(16, quarter), flat(near).astype(bf16), 1, 1)
     for target in range(targets):
         first = target // strips * capacity
-        rows = turned[first : first + capacity]
-        rows = jnp.concatenate([rows, jnp.zeros((height - capacity, rows.shape[1]), f32)], axis=0)
-        message[target] = rows.astype(bf16)
+        message[target] = turned[first : first + capacity].astype(bf16)
 
 
 def finish_body(
@@ -320,7 +318,7 @@
         ],
         name="pack",
         interpret=interpret,
-        compiler_params=pltpu.CompilerParams(vmem_limit_bytes=4 << 20),
+        compiler_params=pltpu.CompilerParams(vmem_limit_bytes=60 << 20),
     )(pixels, upstream)
     gathered = exchange(outgoing, "strip")
 
@@ -362,12 +360,10 @@
         inputs=4,
     )(strip_scalar, gathered, residual, weight, turned)
 
-    returned = [
-        lax.ppermute(result, "strip", [(i, (i + ahead) % strips) for i in range(strips)])
-        if ahead
-        else result
-        for ahead, result in enumerate(results)
-    ]
+    returned = [results[0]]
+    for ahead in range(1, strips):
+        pairs = [(i, (i + ahead) % strips) for i in range(strips)]
+        returned.append(lax.ppermute(results[ahead], "strip", pairs))
 
     by_chip = call(
         functools.partial(turn_body, quarter=quarter),
@@ -384,7 +380,6 @@
     )(strip_scalar, by_chip, slots)
     near = exchange(message, ("line", "group"))
 
-    near, *returned = lax.optimization_barrier((near, *returned))
     output, grad_input = call(
         functools.partial(collect_body, quarter=quarter),
         [jax.ShapeDtypeStruct((channels, width), bf16)] * 2,
@@ -395,7 +390,7 @@
     far = lax.ppermute(near, "core", swap)
     owned_rows = call(
         functools.partial(owned_body, quarter=quarter, capacity=capacity, strips=strips),
-        jax.ShapeDtypeStruct((cores * strips, 8, padded), bf16),
+        jax.ShapeDtypeStruct((cores * strips, capacity, padded), bf16),
     )(near)
     owned_rows = exchange(owned_rows, ("core", "strip"))
     new_weight, new_master, new_first, new_second = call(

time: 108 us -> 112 us (1.037)
  blocking collectives: 0 us -> 19 us
  waiting for transfers between devices: 38.4 us -> 26.4 us
  local copies, waits for them, and re-layouts: 4.02 us -> 2.21 us
    all_to_all x0 -> x1, blocking collectives: none -> 19 us  [exchange(): return lax.all_to_all(value, axes, 0, 0, tiled=True)]
    all_to_all x4 -> x3, waiting for transfers between devices: 27.9 us -> 19.7 us  [exchange(): return lax.all_to_all(value, axes, 0, 0, tiled=True)]
    all_to_all x4 -> x3, starting transfers between devices: 33.5 us -> 25.7 us  [exchange(): return lax.all_to_all(value, axes, 0, 0, tiled=True)]
    ppermute x3, waiting for transfers between devices: 9.25 us -> 5.45 us  [local(): returned.append(lax.ppermute(results[ahead], 'strip', pairs))]
    ppermute x3, starting transfers between devices: 10.9 us -> 14.5 us  [local(): returned.append(lax.ppermute(results[ahead], 'strip', pairs))]
    ppermute x1, starting transfers between devices: 2.47 us -> 5.76 us  [local(): far = lax.ppermute(near, 'core', swap)]
    unnamed x19 -> x15, local copies, waits for them, and re-layouts: 3.32 us -> 1.5 us
  transfers between devices with their start and end apart: 9 -> 8, of which waited for: 7 -> 5; matrix products, arithmetic and copies ran while one was open for 2% -> 2% of each run, Pallas kernels for 3% -> 3%
where the time goes in v2:
time: 112 us; the launch traced here: 111 us
  starting transfers between devices  52.3 us (47%)
  waiting for transfers between devices  26.4 us (24%)
  blocking collectives  19 us (17%)
  Pallas kernels  9.07 us (8%)
  local copies, waits for them, and re-layouts  2.21 us (2%)
  other arithmetic  1.51 us (1%)
    all_to_all x3, starting transfers between devices, exchange(): return lax.all_to_all(value, axes, 0, 0, tiled=True)  25.7 us
    all_to_all x3, waiting for transfers between devices, exchange(): return lax.all_to_all(value, axes, 0, 0, tiled=True)  19.7 us
    all_to_all x1, blocking collectives, exchange(): return lax.all_to_all(value, axes, 0, 0, tiled=True)  19 us
    ppermute x3, starting transfers between devices, local(): returned.append(lax.ppermute(results[ahead], 'strip', pairs))  14.5 us
    ppermute x1, starting transfers between devices, local(): swapped = lax.ppermute(sent, 'core', swap)  6.29 us
    ppermute x1, starting transfers between devices, local(): far = lax.ppermute(near, 'core', swap)  5.76 us
    ppermute x3, waiting for transfers between devices, local(): returned.append(lax.ppermute(results[ahead], 'strip', pairs))  5.45 us
  transfers between devices with their start and end apart: 8, of which 5 were waited for; matrix products, arithmetic and copies ran while one was open for 2% of the time, Pallas kernels for 3%

profile of v2, /device:TPU:1, one launch (start us, length us, event | category | flops | bytes accessed | tf_op | source)
XLA Modules:
  0.0 111.2 jit_solution(16264695599788670587)
XLA Ops:
  0.6 1.7 %pack.1 = bf16[4,400,128]{2,1,0:T(8,128)(2,1)} custom-call(bf16[320,128]{1,0:T(8,128)(2,1)} %bitcast.10, bf16[320,128]{1,0:T(8,128)(2,1)} %bitcast.12), custom_call_target="tpu_custom_call" | custom-call | tf_op jit(solution)/shard_map/pack/pallas_call | solution.py:311
  2.4 11.0 %all-to-all-start = ((bf16[4,400,128]{2,1,0:T(8,128)(2,1)}), bf16[4,400,128]{2,1,0:T(8,128)(2,1)S(1)}, u32[]{:S(2)}, u32[]{:S(2)}) async-start(bf16[4,400,128]{2,1,0:T(8,128)(2,1)} %pack.1), calls=%async_computation | async-start | bytes 819200 | tf_op jit(solution)/shard_map/all_to_all | solution.py:287
  13.4 0.7 copy-done.6
  14.1 0.2 convert_reduce_fusion
  14.3 0.6 convert_reduce_fusion.1
  14.9 0.1 reshape.40
  15.0 0.4 copy.17
  15.4 0.4 copy.18
  15.8 0.4 copy-done.3
  16.2 0.1 shard_map.118.pieces
  16.3 0.7 fusion.1.filled
  17.0 6.5 %all-to-all-done.gathered = bf16[4,400,128]{2,1,0:T(8,128)(2,1)S(1)} async-done(((bf16[4,400,128]{2,1,0:T(8,128)(2,1)}), bf16[4,400,128]{2,1,0:T(8,128)(2,1)S(1)}, u32[]{:S(2)}, u32[]{:S(2)}) %all-to-all-start) | async-done | bytes 409632 | tf_op jit(solution)/shard_map/all_to_all | solution.py:287
  23.5 1.5 %shard_map.121 = (bf16[104,1536]{1,0:T(8,128)(2,1)S(1)}, bf16[104,1536]{1,0:T(8,128)(2,1)S(1)}) custom-call(s32[1]{0:T(128)} %bitcast.8.core, bf16[4,400,128]{2,1,0:T(8,128)(2,1)S(1)} %all-to-all-done.gathered, bf16[2,24,1536]{2,1,0:T(8,128)(2,1)S(1)} %shard_map.118.pieces), custom_call_target="tpu_custom_call" | custom-call | tf_op jit(solution)/shard_map/pallas_call | solution.py:341
  25.0 6.3 %collective-permute-start.3 = (bf16[104,1536]{1,0:T(8,128)(2,1)S(1)}, bf16[104,1536]{1,0:T(8,128)(2,1)S(1)}, u32[]{:S(2)}, u32[]{:S(2)}) collective-permute-start(bf16[104,1536]{1,0:T(8,128)(2,1)S(1)} %get-tuple-element.33), channel_id=1, source_target_pairs={{0,4},{4,0},{1,5},{5,1},{2,6},{6,2},{3,7},{7,3},{8,12},{12,8},{9,1... | collective-permute-start | bytes 958472 | tf_op jit(solution)/shard_map/ppermute | solution.py:348
  31.3 1.2 %collective-permute-done.3.received = bf16[104,1536]{1,0:T(8,128)(2,1)S(1)} collective-permute-done((bf16[104,1536]{1,0:T(8,128)(2,1)S(1)}, bf16[104,1536]{1,0:T(8,128)(2,1)S(1)}, u32[]{:S(2)}, u32[]{:S(2)}) %collective-permute-start.3) | collective-permute-done | bytes 319520 | tf_op jit(solution)/shard_map/ppermute | solution.py:348
  32.6 0.9 shard_map.122
  33.5 11.4 %all-to-all-start.1 = ((bf16[64,24,128]{2,1,0:T(8,128)(2,1)}), bf16[64,24,128]{2,1,0:T(8,128)(2,1)S(1)}, u32[]{:S(2)}, u32[]{:S(2)}) async-start(bf16[64,24,128]{2,1,0:T(8,128)(2,1)} %shard_map.122), calls=%async_computation.1 | async-start | bytes 786432 | tf_op jit(solution)/shard_map/all_to_all | solution.py:287
  44.9 13.2 %all-to-all-done.1.received = bf16[64,24,128]{2,1,0:T(8,128)(2,1)S(1)} async-done(((bf16[64,24,128]{2,1,0:T(8,128)(2,1)}), bf16[64,24,128]{2,1,0:T(8,128)(2,1)S(1)}, u32[]{:S(2)}, u32[]{:S(2)}) %all-to-all-start.1) | async-done | bytes 393248 | tf_op jit(solution)/shard_map/all_to_all | solution.py:287
  58.1 0.6 shard_map.123
  58.7 19.0 %all_to_all.20.near = bf16[64,24,128]{2,1,0:T(8,128)(2,1)S(1)} all-to-all(bf16[64,24,128]{2,1,0:T(8,128)(2,1)S(1)} %shard_map.123), channel_id=1, replica_groups=mesh['line'=8,'group'=8,'core'=2,'strip'=4] {'line','group'}, dimensions={0} | all-to-all | bytes 786432 | tf_op jit(solution)/shard_map/all_to_all | solution.py:287
  77.7 5.8 %collective-permute-start.4 = (bf16[64,24,128]{2,1,0:T(8,128)(2,1)S(1)}, bf16[64,24,128]{2,1,0:T(8,128)(2,1)S(1)}, u32[]{:S(2)}, u32[]{:S(2)}) collective-permute-start(bf16[64,24,128]{2,1,0:T(8,128)(2,1)S(1)} %all_to_all.20.near), channel_id=1, source_target_pairs={{0,4},{4,0},{1,5},{5,1},{2,6},{6,2},{3,7},{7,3},{8,12},{12,8},{9,1... | collective-permute-start | bytes 1179656 | tf_op jit(solution)/shard_map/ppermute | solution.py:390
  83.5 0.2 copy.19.turned
  83.7 0.9 shard_map.124
  84.6 3.3 %all-to-all-start.3 = ((bf16[8,4,1536]{2,1,0:T(4,128)(2,1)}), bf16[8,4,1536]{2,1,0:T(4,128)(2,1)S(1)}, u32[]{:S(2)}, u32[]{:S(2)}) async-start(bf16[8,4,1536]{2,1,0:T(4,128)(2,1)} %shard_map.124), calls=%async_computation.3 | async-start | bytes 196608 | tf_op jit(solution)/shard_map/all_to_all | solution.py:287
  87.9 1.3 %shard_map.119 = (bf16[400,128]{1,0:T(8,128)(2,1)S(1)}, bf16[400,128]{1,0:T(8,128)(2,1)S(1)}, bf16[400,128]{1,0:T(8,128)(2,1)S(1)}, bf16[400,128]{1,0:T(8,128)(2,1)S(1)}) custom-call(s32[1]{0:T(128)} %bitcast.strip, bf16[4,400,128]{2,1,0:T(8,128)(2,1)S(1)} %all-to-all-done.gathered, bf16[4,80,128]{2,1,0:T(8,128)(2,1)S(1)} %constant_dynamic-slice_fusion.residual, ...), custom_call_target="tpu_custom_call" | custom-call | tf_op jit(solution)/shard_map/pallas_call | solution.py:351
  89.3 4.1 %collective-permute-start = (bf16[400,128]{1,0:T(8,128)(2,1)S(1)}, bf16[400,128]{1,0:T(8,128)(2,1)S(1)}, u32[]{:S(2)}, u32[]{:S(2)}) collective-permute-start(bf16[400,128]{1,0:T(8,128)(2,1)S(1)} %get-tuple-element.26), channel_id=1, source_target_pairs={{0,1},{1,2},{2,3},{3,0},{4,5},{5,6},{6,7},{7,4},{8,9},{9,10},{10,1... | collective-permute-start | bytes 307208 | tf_op jit(solution)/shard_map/ppermute | solution.py:366
  93.4 5.2 %collective-permute-start.1 = (bf16[400,128]{1,0:T(8,128)(2,1)S(1)}, bf16[400,128]{1,0:T(8,128)(2,1)S(1)}, u32[]{:S(2)}, u32[]{:S(2)}) collective-permute-start(bf16[400,128]{1,0:T(8,128)(2,1)S(1)} %get-tuple-element.27), channel_id=1, source_target_pairs={{0,2},{1,3},{2,0},{3,1},{4,6},{5,7},{6,4},{7,5},{8,10},{9,11},{10,... | collective-permute-start | bytes 307208 | tf_op jit(solution)/shard_map/ppermute | solution.py:366
  98.6 5.2 %collective-permute-start.2 = (bf16[400,128]{1,0:T(8,128)(2,1)S(1)}, bf16[400,128]{1,0:T(8,128)(2,1)S(1)}, u32[]{:S(2)}, u32[]{:S(2)}) collective-permute-start(bf16[400,128]{1,0:T(8,128)(2,1)S(1)} %get-tuple-element.28), channel_id=1, source_target_pairs={{0,3},{1,0},{2,1},{3,2},{4,7},{5,4},{6,5},{7,6},{8,11},{9,8},{10,9... | collective-permute-start | bytes 307208 | tf_op jit(solution)/shard_map/ppermute | solution.py:366
  103.8 2.2 %collective-permute-done.1.pieces_2_ = bf16[400,128]{1,0:T(8,128)(2,1)S(1)} collective-permute-done((bf16[400,128]{1,0:T(8,128)(2,1)S(1)}, bf16[400,128]{1,0:T(8,128)(2,1)S(1)}, u32[]{:S(2)}, u32[]{:S(2)}) %collective-permute-start.1) | collective-permute-done | bytes 102432 | tf_op jit(solution)/shard_map/ppermute | solution.py:366
  106.1 3.2 %collective-permute-done.2.pieces_3_ = bf16[400,128]{1,0:T(8,128)(2,1)S(1)} collective-permute-done((bf16[400,128]{1,0:T(8,128)(2,1)S(1)}, bf16[400,128]{1,0:T(8,128)(2,1)S(1)}, u32[]{:S(2)}, u32[]{:S(2)}) %collective-permute-start.2) | collective-permute-done | bytes 102432 | tf_op jit(solution)/shard_map/ppermute | solution.py:366
  109.3 0.8 shard_map.120
  110.1 1.2 %shard_map.125 = (bf16[80,2880]{1,0:T(8,128)(2,1)}, f32[4,2880]{1,0:T(4,128)}, f32[4,2880]{1,0:T(4,128)}, f32[4,2880]{1,0:T(4,128)}) custom-call(s32[1]{0:T(128)} %bitcast.8.core, bf16[64,24,128]{2,1,0:T(8,128)(2,1)S(1)} %all_to_all.20.near, bf16[64,24,128]{2,1,0:T(8,128)(2,1)S(1)} %collective-permute-done.4.far, ...), custom_call_target="tpu_custom_call" | custom-call | tf_op jit(solution)/shard_map/pallas_call | solution.py:396
  (17 shorter events, 0.1 us)
Async XLA Ops:
  2.4 12.6 %copy-start = (bf16[80,2880]{1,0:T(8,128)(2,1)S(1)}, bf16[80,2880]{1,0:T(8,128)(2,1)}, u32[]{:S(2)}) copy-start(bf16[80,2880]{1,0:T(8,128)(2,1)} %weight.1) | copy-start | bytes 1382404
  2.4 21.1 %all-to-all-start = ((bf16[4,400,128]{2,1,0:T(8,128)(2,1)}), bf16[4,400,128]{2,1,0:T(8,128)(2,1)S(1)}, u32[]{:S(2)}, u32[]{:S(2)}) async-start(bf16[4,400,128]{2,1,0:T(8,128)(2,1)} %pack.1), calls=%async_computation | async-start | bytes 819200 | tf_op jit(solution)/shard_map/all_to_all | solution.py:287
  13.4 0.7 copy-start.6
  15.4 0.8 copy-start.3
  15.4 0.8 copy-start.4
  15.4 0.8 copy-start.5
  25.0 7.5 %collective-permute-start.3 = (bf16[104,1536]{1,0:T(8,128)(2,1)S(1)}, bf16[104,1536]{1,0:T(8,128)(2,1)S(1)}, u32[]{:S(2)}, u32[]{:S(2)}) collective-permute-start(bf16[104,1536]{1,0:T(8,128)(2,1)S(1)} %get-tuple-element.33), channel_id=1, source_target_pairs={{0,4},{4,0},{1,5},{5,1},{2,6},{6,2},{3,7},{7,3},{8,12},{12,8},{9,1... | collective-permute-start | bytes 958472 | tf_op jit(solution)/shard_map/ppermute | solution.py:348
  33.5 24.6 %all-to-all-start.1 = ((bf16[64,24,128]{2,1,0:T(8,128)(2,1)}), bf16[64,24,128]{2,1,0:T(8,128)(2,1)S(1)}, u32[]{:S(2)}, u32[]{:S(2)}) async-start(bf16[64,24,128]{2,1,0:T(8,128)(2,1)} %shard_map.122), calls=%async_computation.1 | async-start | bytes 786432 | tf_op jit(solution)/shard_map/all_to_all | solution.py:287
  77.7 32.3 %collective-permute-start.4 = (bf16[64,24,128]{2,1,0:T(8,128)(2,1)S(1)}, bf16[64,24,128]{2,1,0:T(8,128)(2,1)S(1)}, u32[]{:S(2)}, u32[]{:S(2)}) collective-permute-start(bf16[64,24,128]{2,1,0:T(8,128)(2,1)S(1)} %all_to_all.20.near), channel_id=1, source_target_pairs={{0,4},{4,0},{1,5},{5,1},{2,6},{6,2},{3,7},{7,3},{8,12},{12,8},{9,1... | collective-permute-start | bytes 1179656 | tf_op jit(solution)/shard_map/ppermute | solution.py:390
  84.6 25.5 %all-to-all-start.3 = ((bf16[8,4,1536]{2,1,0:T(4,128)(2,1)}), bf16[8,4,1536]{2,1,0:T(4,128)(2,1)S(1)}, u32[]{:S(2)}, u32[]{:S(2)}) async-start(bf16[8,4,1536]{2,1,0:T(4,128)(2,1)} %shard_map.124), calls=%async_computation.3 | async-start | bytes 196608 | tf_op jit(solution)/shard_map/all_to_all | solution.py:287
  87.9 21.4 %copy-start.1 = (bf16[1,1,320,128]{3,2,1,0:T(8,128)(2,1)S(1)}, bf16[1,1,320,128]{3,2,1,0:T(8,128)(2,1)}, u32[]{:S(2)}) copy-start(bf16[1,1,320,128]{3,2,1,0:T(8,128)(2,1)} %param.7) | copy-start | bytes 245764
  87.9 21.4 %copy-start.2 = (bf16[1,1,320,128]{3,2,1,0:T(8,128)(2,1)S(1)}, bf16[1,1,320,128]{3,2,1,0:T(8,128)(2,1)}, u32[]{:S(2)}) copy-start(bf16[1,1,320,128]{3,2,1,0:T(8,128)(2,1)} %param.8) | copy-start | bytes 245764
  89.3 14.6 %collective-permute-start = (bf16[400,128]{1,0:T(8,128)(2,1)S(1)}, bf16[400,128]{1,0:T(8,128)(2,1)S(1)}, u32[]{:S(2)}, u32[]{:S(2)}) collective-permute-start(bf16[400,128]{1,0:T(8,128)(2,1)S(1)} %get-tuple-element.26), channel_id=1, source_target_pairs={{0,1},{1,2},{2,3},{3,0},{4,5},{5,6},{6,7},{7,4},{8,9},{9,10},{10,1... | collective-permute-start | bytes 307208 | tf_op jit(solution)/shard_map/ppermute | solution.py:366
  93.4 12.7 %collective-permute-start.1 = (bf16[400,128]{1,0:T(8,128)(2,1)S(1)}, bf16[400,128]{1,0:T(8,128)(2,1)S(1)}, u32[]{:S(2)}, u32[]{:S(2)}) collective-permute-start(bf16[400,128]{1,0:T(8,128)(2,1)S(1)} %get-tuple-element.27), channel_id=1, source_target_pairs={{0,2},{1,3},{2,0},{3,1},{4,6},{5,7},{6,4},{7,5},{8,10},{9,11},{10,... | collective-permute-start | bytes 307208 | tf_op jit(solution)/shard_map/ppermute | solution.py:366
  98.6 10.7 %collective-permute-start.2 = (bf16[400,128]{1,0:T(8,128)(2,1)S(1)}, bf16[400,128]{1,0:T(8,128)(2,1)S(1)}, u32[]{:S(2)}, u32[]{:S(2)}) collective-permute-start(bf16[400,128]{1,0:T(8,128)(2,1)S(1)} %get-tuple-element.28), channel_id=1, source_target_pairs={{0,3},{1,0},{2,1},{3,2},{4,7},{5,4},{6,5},{7,6},{8,11},{9,8},{10,9... | collective-permute-start | bytes 307208 | tf_op jit(solution)/shard_map/ppermute | solution.py:366

commit v3 on v2

--- a/solution.py
+++ b/solution.py
@@ -15,7 +15,7 @@
 
 interpret = False
 LANES = 128
-RANK_SHAPE = (8, 8, 2)
+RANK_SHAPE = (8, 4, 2, 2)
 TERMS = 2
 taps = [(dh, dw) for dh in (-1, 0, 1) for dw in (-1, 0, 1)]
 f32 = jnp.float32
@@ -184,21 +184,23 @@
     return master - update, first_new, second_new
 
 
-def publish_body(strip, received, slots, message, *, quarter, capacity, cores, root):
+def publish_body(strip, received, slots, message, *, quarter, capacity, halves, cores, root):
     chips, chunk, _ = received.shape
+    places = message.shape[0]
     strips = slots.shape[0]
     columns = max(LANES, chips * cores * capacity)
     mine = slots[0:1, :]
     for other in range(1, strips):
         mine = jnp.where(strip[0] == other, slots[other : other + 1, :], mine)
     wide = jnp.concatenate([mine] * 3, axis=1)
-    owner, place = wide // capacity, wide % capacity
+    owner, slot = wide // capacity, wide % capacity
+    source = owner // cores % halves * places + owner // (halves * cores)
     share = TERMS * 3 * capacity
     row = lax.broadcasted_iota(jnp.int32, (LANES, 3 * LANES), 0) - quarter
     array = lax.broadcasted_iota(jnp.int32, (LANES, 3 * LANES), 1) // LANES
     within = row % (3 * capacity)
     here = (row >= 0) & (row < cores * share) & (wide >= 0) & (row // share == owner % cores)
-    here = here & (within // capacity == array) & (within % capacity == place)
+    here = here & (within // capacity == array) & (within % capacity == slot)
     here = jnp.where(here, 1.0, 0.0).astype(bf16)
     values = [received[chip].astype(f32) for chip in range(chips)]
     grads = values[0]
@@ -207,9 +209,7 @@
     picked = dot(jnp.concatenate(values, axis=0).astype(bf16), here, 1, 0)
     state = jnp.zeros((chunk, 3 * LANES), f32)
     for chip in range(chips):
-        state = jnp.where(
-            owner // cores == chip, picked[chip * chunk : (chip + 1) * chunk], state
-        )
+        state = jnp.where(source == chip, picked[chip * chunk : (chip + 1) * chunk], state)
     fresh, _, _ = adam(
         grads / root, state[:, :LANES], state[:, LANES : 2 * LANES], state[:, 2 * LANES :]
     )
@@ -217,14 +217,14 @@
     matches = jnp.where(index == mine, 1.0, 0.0).astype(bf16)
     chosen = dot(grads.astype(bf16), matches, 1, 1)
     lane = lax.broadcasted_iota(jnp.int32, (chunk, LANES), 1)
-    span = cores * capacity
+    span = halves * cores * capacity
     per_tile = LANES // span
-    for chip in range(chips):
-        tile = chosen[:, chip // per_tile * LANES : (chip // per_tile + 1) * LANES]
-        shift = (quarter - span * (chip % per_tile)) % LANES
+    for place in range(places):
+        tile = chosen[:, place // per_tile * LANES : (place // per_tile + 1) * LANES]
+        shift = (quarter - span * (place % per_tile)) % LANES
         moved = tile if shift == 0 else pltpu.roll(tile, shift, 1)
         value = jnp.where(lane < quarter, fresh, jnp.where(lane < quarter + span, moved, 0.0))
-        message[chip] = value.astype(bf16)
+        message[place] = value.astype(bf16)
 
 
 def flat(messages):
@@ -242,30 +242,50 @@
 
 def owned_body(near, message, *, quarter, capacity, strips):
     targets = message.shape[0]
-    turned = dot(unit(16, quarter), flat(near).astype(bf16), 1, 1)
+    turned = dot(unit(targets // strips * capacity, quarter), flat(near).astype(bf16), 1, 1)
     for target in range(targets):
         first = target // strips * capacity
         message[target] = turned[first : first + capacity].astype(bf16)
 
 
+def valid(blocks, halves, step):
+    size = blocks // halves
+    return [min(size, step - half * size) for half in range(halves)]
+
+
+def collect_weight_body(seat, *refs, halves, step):
+    *shares, new_weight = refs
+    quarter = new_weight.shape[0]
+    seats = len(shares)
+    shares = [flat(share) for share in shares]
+    sizes = valid(shares[0].shape[0] * halves, halves, step)
+    rows = []
+    for core in range(seats // halves):
+        for half in range(halves):
+            target = half * (seats // halves) + core
+            block = shares[0]
+            for other in range(1, seats):
+                block = jnp.where(seat[0] == target ^ other, shares[other], block)
+            rows.append(block[: sizes[half]])
+    rows = jnp.concatenate(rows, axis=0).astype(bf16)
+    new_weight[...] = dot(unit(quarter, 0), rows, 1, 1).astype(bf16)
+
+
 def finish_body(
-    core, near, far, owned, master, first_moment, second_moment, filled,
-    new_weight, new_master, new_first, new_second, *, step, strips, root,
+    owned, master, first_moment, second_moment, filled,
+    new_master, new_first, new_second, *, halves, step, strips, root,
 ):
-    quarter, capacity = new_weight.shape[0], master.shape[0]
-    ours, others = flat(near), flat(far)
-    first = core[0] == 0
-    rows = [jnp.where(first, ours, others)[:step], jnp.where(first, others, ours)[:step]]
-    rows = jnp.concatenate(rows, axis=0).astype(bf16)
-    turned = dot(unit(quarter, 0), rows, 1, 1)
-    new_weight[...] = turned.astype(bf16)
-    halves = []
-    for half in range(owned.shape[0] // strips):
-        total = owned[half * strips].astype(f32)
-        for strip in range(1, strips):
-            total = total + owned[half * strips + strip].astype(f32)
-        halves.append(total[:capacity, :step])
-    grads = jnp.concatenate(halves, axis=1) / root
+    seats, size = owned.shape[0] // strips, owned.shape[2]
+    sizes = valid(size * halves, halves, step)
+    blocks = []
+    for core in range(seats // halves):
+        for half in range(halves):
+            first = (half * (seats // halves) + core) * strips
+            total = owned[first].astype(f32)
+            for strip in range(1, strips):
+                total = total + owned[first + strip].astype(f32)
+            blocks.append(total[:, : sizes[half]])
+    grads = jnp.concatenate(blocks, axis=1) / root
     fresh, first_new, second_new = adam(
         grads, master[...], first_moment[...], second_moment[...]
     )
@@ -288,11 +308,16 @@
 
 
 def local(latents, cotangent, weight, master, first_moment, second_moment, owner_list):
-    lines, groups, cores, strips = (lax.axis_size(a) for a in ("line", "group", "core", "strip"))
-    chips = lines * groups
+    lines, columns, halves, cores, strips = (
+        lax.axis_size(axis) for axis in ("line", "column", "half", "core", "strip")
+    )
+    places = lines * columns
+    seats = halves * cores
+    chips = places * halves
     ranks = chips * cores
     strip, core = lax.axis_index("strip"), lax.axis_index("core")
-    rank = (lax.axis_index("line") * groups + lax.axis_index("group")) * cores + core
+    seat = lax.axis_index("half") * cores + core
+    rank = (lax.axis_index("line") * columns + lax.axis_index("column")) * seats + seat
     strip_scalar = strip.reshape(1).astype(jnp.int32)
     core_scalar = core.reshape(1).astype(jnp.int32)
     swap = [(i, cores - 1 - i) for i in range(cores)]
@@ -371,14 +396,17 @@
         scalars=1,
         inputs=2,
     )(core_scalar, kept, swapped)
-    by_chip = exchange(by_chip, ("line", "group"))
+    by_chip = exchange(by_chip, ("half", "line", "column"))
     message = call(
-        functools.partial(publish_body, quarter=quarter, capacity=capacity, cores=cores, root=root),
-        jax.ShapeDtypeStruct((chips, chunk, LANES), bf16),
+        functools.partial(
+            publish_body, quarter=quarter, capacity=capacity, halves=halves, cores=cores,
+            root=root,
+        ),
+        jax.ShapeDtypeStruct((places, chunk, LANES), bf16),
         scalars=1,
         inputs=2,
     )(strip_scalar, by_chip, slots)
-    near = exchange(message, ("line", "group"))
+    near = exchange(message, ("line", "column"))
 
     output, grad_input = call(
         functools.partial(collect_body, quarter=quarter),
@@ -387,28 +415,34 @@
         inputs=2 + strips,
     )(strip_scalar, pixels, upstream, *returned)
 
-    far = lax.ppermute(near, "core", swap)
+    shares = [near]
+    for other in range(1, seats):
+        pairs = [(i, i ^ other) for i in range(seats)]
+        shares.append(lax.ppermute(near, ("half", "core"), pairs))
     owned_rows = call(
         functools.partial(owned_body, quarter=quarter, capacity=capacity, strips=strips),
-        jax.ShapeDtypeStruct((cores * strips, capacity, padded), bf16),
+        jax.ShapeDtypeStruct((seats * strips, capacity, places * chunk), bf16),
     )(near)
-    owned_rows = exchange(owned_rows, ("core", "strip"))
-    new_weight, new_master, new_first, new_second = call(
-        functools.partial(finish_body, step=step, strips=strips, root=root),
-        [jax.ShapeDtypeStruct((quarter, taken), bf16)]
-        + [jax.ShapeDtypeStruct(master.shape, f32)] * 3,
-        scalars=1,
-        inputs=7,
-    )(core_scalar, near, far, owned_rows, master, first_moment, second_moment, filled)
+    owned_rows = exchange(owned_rows, ("half", "core", "strip"))
+    new_weight = call(
+        functools.partial(collect_weight_body, halves=halves, step=step),
+        jax.ShapeDtypeStruct((quarter, taken), bf16),
+        scalars=1,
+        inputs=seats,
+    )(seat.reshape(1).astype(jnp.int32), *shares)
+    new_master, new_first, new_second = call(
+        functools.partial(finish_body, halves=halves, step=step, strips=strips, root=root),
+        [jax.ShapeDtypeStruct(master.shape, f32)] * 3,
+    )(owned_rows, master, first_moment, second_moment, filled)
     return (output[None, None], grad_input[None, None], new_weight, new_master, new_first, new_second)
 
 
 def solution(mesh):
     fine = Mesh(
         mesh.devices.reshape(RANK_SHAPE + (mesh.shape["strip"],)),
-        ("line", "group", "core", "strip"),
-    )
-    ranks = ("line", "group", "core")
+        ("line", "column", "half", "core", "strip"),
+    )
+    ranks = ("line", "column", "half", "core")
     images = P(ranks, "strip", None, None)
     specs = (images, images, P("strip", None), P(ranks, None), P(ranks, None), P(ranks, None))
 

time: 112 us -> 112 us (level)
  blocking collectives: 19 us -> 0 us
  starting transfers between devices: 52.3 us -> 61 us
  waiting for transfers between devices: 26.4 us -> 34.7 us
  Pallas kernels: 9.07 us -> 10.5 us
    all_to_all x1 -> x0, blocking collectives: 19 us -> none  [exchange(): return lax.all_to_all(value, axes, 0, 0, tiled=True)]
    all_to_all x3 -> x4, starting transfers between devices: 25.7 us -> 32.3 us  [exchange(): return lax.all_to_all(value, axes, 0, 0, tiled=True)]
    all_to_all x3 -> x4, waiting for transfers between devices: 19.7 us -> 25.4 us  [exchange(): return lax.all_to_all(value, axes, 0, 0, tiled=True)]
    ppermute x1 -> x3, starting transfers between devices: 5.76 us -> 10.4 us  [local(): shares.append(lax.ppermute(near, ('half', 'core'), pairs))]
    ppermute x3, waiting for transfers between devices: 5.45 us -> 8.16 us  [local(): returned.append(lax.ppermute(results[ahead], 'strip', pairs))]
    ppermute x3, starting transfers between devices: 14.5 us -> 12 us  [local(): returned.append(lax.ppermute(results[ahead], 'strip', pairs))]
  transfers between devices with their start and end apart: 8 -> 11, of which waited for: 5 -> 6; matrix products, arithmetic and copies ran while one was open for 2% -> 2% of each run, Pallas kernels for 3% -> 3%
where the time goes in v3:
time: 112 us; the launch traced here: 111 us
  starting transfers between devices  61 us (54%)
  waiting for transfers between devices  34.7 us (31%)
  Pallas kernels  10.5 us (9%)
  local copies, waits for them, and re-layouts  2.25 us (2%)
  other arithmetic  1.51 us (1%)
    all_to_all x4, starting transfers between devices, exchange(): return lax.all_to_all(value, axes, 0, 0, tiled=True)  32.3 us
    all_to_all x4, waiting for transfers between devices, exchange(): return lax.all_to_all(value, axes, 0, 0, tiled=True)  25.4 us
    ppermute x3, starting transfers between devices, local(): returned.append(lax.ppermute(results[ahead], 'strip', pairs))  12 us
    ppermute x3, starting transfers between devices, local(): shares.append(lax.ppermute(near, ('half', 'core'), pairs))  10.4 us
    ppermute x3, waiting for transfers between devices, local(): returned.append(lax.ppermute(results[ahead], 'strip', pairs))  8.16 us
    ppermute x1, starting transfers between devices, local(): swapped = lax.ppermute(sent, 'core', swap)  6.29 us
  transfers between devices with their start and end apart: 11, of which 6 were waited for; matrix products, arithmetic and copies ran while one was open for 2% of the time, Pallas kernels for 3%

profile of v3, /device:TPU:1, one launch (start us, length us, event | category | flops | bytes accessed | tf_op | source)
XLA Modules:
  0.0 110.8 jit_solution(4663618403883565234)
XLA Ops:
  0.6 1.7 %pack.1 = bf16[4,400,128]{2,1,0:T(8,128)(2,1)} custom-call(bf16[320,128]{1,0:T(8,128)(2,1)} %bitcast.11, bf16[320,128]{1,0:T(8,128)(2,1)} %bitcast.13), custom_call_target="tpu_custom_call" | custom-call | tf_op jit(solution)/shard_map/pack/pallas_call | solution.py:336
  2.4 11.0 %all-to-all-start = ((bf16[4,400,128]{2,1,0:T(8,128)(2,1)}), bf16[4,400,128]{2,1,0:T(8,128)(2,1)S(1)}, u32[]{:S(2)}, u32[]{:S(2)}) async-start(bf16[4,400,128]{2,1,0:T(8,128)(2,1)} %pack.1), calls=%async_computation | async-start | bytes 819200 | tf_op jit(solution)/shard_map/all_to_all | solution.py:307
  13.4 0.7 copy-done.6
  14.3 0.6 convert_reduce_fusion.1
  15.0 0.4 copy.17
  15.4 0.4 copy.18
  15.8 0.4 copy-done.3
  16.4 0.7 fusion.1.filled
  17.0 6.4 %all-to-all-done.gathered = bf16[4,400,128]{2,1,0:T(8,128)(2,1)S(1)} async-done(((bf16[4,400,128]{2,1,0:T(8,128)(2,1)}), bf16[4,400,128]{2,1,0:T(8,128)(2,1)S(1)}, u32[]{:S(2)}, u32[]{:S(2)}) %all-to-all-start) | async-done | bytes 409632 | tf_op jit(solution)/shard_map/all_to_all | solution.py:307
  23.5 1.5 %shard_map.121 = (bf16[104,1536]{1,0:T(8,128)(2,1)S(1)}, bf16[104,1536]{1,0:T(8,128)(2,1)S(1)}) custom-call(s32[1]{0:T(128)} %bitcast.9.core, bf16[4,400,128]{2,1,0:T(8,128)(2,1)S(1)} %all-to-all-done.gathered, bf16[2,24,1536]{2,1,0:T(8,128)(2,1)S(1)} %shard_map.118.pieces), custom_call_target="tpu_custom_call" | custom-call | tf_op jit(solution)/shard_map/pallas_call | solution.py:366
  25.0 6.3 %collective-permute-start.3 = (bf16[104,1536]{1,0:T(8,128)(2,1)S(1)}, bf16[104,1536]{1,0:T(8,128)(2,1)S(1)}, u32[]{:S(2)}, u32[]{:S(2)}) collective-permute-start(bf16[104,1536]{1,0:T(8,128)(2,1)S(1)} %get-tuple-element.32), channel_id=1, source_target_pairs={{0,4},{4,0},{1,5},{5,1},{2,6},{6,2},{3,7},{7,3},{8,12},{12,8},{9,1... | collective-permute-start | bytes 958472 | tf_op jit(solution)/shard_map/ppermute | solution.py:373
  31.3 1.2 %collective-permute-done.3.received = bf16[104,1536]{1,0:T(8,128)(2,1)S(1)} collective-permute-done((bf16[104,1536]{1,0:T(8,128)(2,1)S(1)}, bf16[104,1536]{1,0:T(8,128)(2,1)S(1)}, u32[]{:S(2)}, u32[]{:S(2)}) %collective-permute-start.3) | collective-permute-done | bytes 319520 | tf_op jit(solution)/shard_map/ppermute | solution.py:373
  32.6 0.9 shard_map.122
  33.5 11.4 %all-to-all-start.1 = ((bf16[64,24,128]{2,1,0:T(8,128)(2,1)}), bf16[64,24,128]{2,1,0:T(8,128)(2,1)S(1)}, u32[]{:S(2)}, u32[]{:S(2)}) async-start(bf16[64,24,128]{2,1,0:T(8,128)(2,1)} %shard_map.122), calls=%async_computation.1 | async-start | bytes 786432 | tf_op jit(solution)/shard_map/all_to_all | solution.py:307
  44.9 13.2 %all-to-all-done.1.received = bf16[64,24,128]{2,1,0:T(8,128)(2,1)S(1)} async-done(((bf16[64,24,128]{2,1,0:T(8,128)(2,1)}), bf16[64,24,128]{2,1,0:T(8,128)(2,1)S(1)}, u32[]{:S(2)}, u32[]{:S(2)}) %all-to-all-start.1) | async-done | bytes 393248 | tf_op jit(solution)/shard_map/all_to_all | solution.py:307
  58.0 1.3 %shard_map.123 = bf16[32,24,128]{2,1,0:T(8,128)(2,1)} custom-call(s32[1]{0:T(128)} %bitcast.strip, bf16[64,24,128]{2,1,0:T(8,128)(2,1)S(1)} %all-to-all-done.1.received, s32[4,128]{1,0:T(4,128)S(1)} %pad.4.slots), custom_call_target="tpu_custom_call" | custom-call | tf_op jit(solution)/shard_map/pallas_call | solution.py:400
  59.3 6.3 %all-to-all-start.2 = ((bf16[32,24,128]{2,1,0:T(8,128)(2,1)}), bf16[32,24,128]{2,1,0:T(8,128)(2,1)S(1)}, u32[]{:S(2)}, u32[]{:S(2)}) async-start(bf16[32,24,128]{2,1,0:T(8,128)(2,1)} %shard_map.123), calls=%async_computation.2 | async-start | bytes 393216 | tf_op jit(solution)/shard_map/all_to_all | solution.py:307
  65.9 1.3 %shard_map.119 = (bf16[400,128]{1,0:T(8,128)(2,1)S(1)}, bf16[400,128]{1,0:T(8,128)(2,1)S(1)}, bf16[400,128]{1,0:T(8,128)(2,1)S(1)}, bf16[400,128]{1,0:T(8,128)(2,1)S(1)}) custom-call(s32[1]{0:T(128)} %bitcast.strip, bf16[4,400,128]{2,1,0:T(8,128)(2,1)S(1)} %all-to-all-done.gathered, bf16[4,80,128]{2,1,0:T(8,128)(2,1)S(1)} %constant_dynamic-slice_fusion.residual, ...), custom_call_target="tpu_custom_call" | custom-call | tf_op jit(solution)/shard_map/pallas_call | solution.py:376
  67.2 2.6 %collective-permute-start = (bf16[400,128]{1,0:T(8,128)(2,1)S(1)}, bf16[400,128]{1,0:T(8,128)(2,1)S(1)}, u32[]{:S(2)}, u32[]{:S(2)}) collective-permute-start(bf16[400,128]{1,0:T(8,128)(2,1)S(1)} %get-tuple-element.25), channel_id=1, source_target_pairs={{0,1},{1,2},{2,3},{3,0},{4,5},{5,6},{6,7},{7,4},{8,9},{9,10},{10,1... | collective-permute-start | bytes 307208 | tf_op jit(solution)/shard_map/ppermute | solution.py:391
  69.8 5.7 %all-to-all-done.2.refs_0_.near = bf16[32,24,128]{2,1,0:T(8,128)(2,1)S(1)} async-done(((bf16[32,24,128]{2,1,0:T(8,128)(2,1)}), bf16[32,24,128]{2,1,0:T(8,128)(2,1)S(1)}, u32[]{:S(2)}, u32[]{:S(2)}) %all-to-all-start.2) | async-done | bytes 196640 | tf_op jit(solution)/shard_map/all_to_all | solution.py:307
  75.6 4.9 %collective-permute-start.4 = (bf16[32,24,128]{2,1,0:T(8,128)(2,1)S(1)}, bf16[32,24,128]{2,1,0:T(8,128)(2,1)S(1)}, u32[]{:S(2)}, u32[]{:S(2)}) collective-permute-start(bf16[32,24,128]{2,1,0:T(8,128)(2,1)S(1)} %all-to-all-done.2.refs_0_.near), channel_id=1, source_target_pairs={{0,4},{4,0},{8,12},{12,8},{1,5},{5,1},{9,13},{13,9},{2,6},{6,2},{1... | collective-permute-start | bytes 589832 | tf_op jit(solution)/shard_map/ppermute | solution.py:421
  80.5 2.2 %collective-permute-start.5 = (bf16[32,24,128]{2,1,0:T(8,128)(2,1)S(1)}, bf16[32,24,128]{2,1,0:T(8,128)(2,1)S(1)}, u32[]{:S(2)}, u32[]{:S(2)}) collective-permute-start(bf16[32,24,128]{2,1,0:T(8,128)(2,1)S(1)} %all-to-all-done.2.refs_0_.near), channel_id=1, source_target_pairs={{0,8},{4,12},{8,0},{12,4},{1,9},{5,13},{9,1},{13,5},{2,10},{6,14},... | collective-permute-start | bytes 589832 | tf_op jit(solution)/shard_map/ppermute | solution.py:421
  82.7 3.3 %collective-permute-start.6 = (bf16[32,24,128]{2,1,0:T(8,128)(2,1)S(1)}, bf16[32,24,128]{2,1,0:T(8,128)(2,1)S(1)}, u32[]{:S(2)}, u32[]{:S(2)}) collective-permute-start(bf16[32,24,128]{2,1,0:T(8,128)(2,1)S(1)} %all-to-all-done.2.refs_0_.near), channel_id=1, source_target_pairs={{0,12},{4,8},{8,4},{12,0},{1,13},{5,9},{9,5},{13,1},{2,14},{6,10},... | collective-permute-start | bytes 589832 | tf_op jit(solution)/shard_map/ppermute | solution.py:421
  86.0 0.8 shard_map.125
  86.8 3.7 %all-to-all-start.3 = ((bf16[16,4,768]{2,1,0:T(4,128)(2,1)}), bf16[16,4,768]{2,1,0:T(4,128)(2,1)S(1)}, u32[]{:S(2)}, u32[]{:S(2)}) async-start(bf16[16,4,768]{2,1,0:T(4,128)(2,1)} %shard_map.125), calls=%async_computation.3 | async-start | bytes 196608 | tf_op jit(solution)/shard_map/all_to_all | solution.py:307
  90.5 7.2 %collective-permute-start.1 = (bf16[400,128]{1,0:T(8,128)(2,1)S(1)}, bf16[400,128]{1,0:T(8,128)(2,1)S(1)}, u32[]{:S(2)}, u32[]{:S(2)}) collective-permute-start(bf16[400,128]{1,0:T(8,128)(2,1)S(1)} %get-tuple-element.26), channel_id=1, source_target_pairs={{0,2},{1,3},{2,0},{3,1},{4,6},{5,7},{6,4},{7,5},{8,10},{9,11},{10,... | collective-permute-start | bytes 307208 | tf_op jit(solution)/shard_map/ppermute | solution.py:391
  97.7 2.2 %collective-permute-start.2 = (bf16[400,128]{1,0:T(8,128)(2,1)S(1)}, bf16[400,128]{1,0:T(8,128)(2,1)S(1)}, u32[]{:S(2)}, u32[]{:S(2)}) collective-permute-start(bf16[400,128]{1,0:T(8,128)(2,1)S(1)} %get-tuple-element.27), channel_id=1, source_target_pairs={{0,3},{1,0},{2,1},{3,2},{4,7},{5,4},{6,5},{7,6},{8,11},{9,8},{10,9... | collective-permute-start | bytes 307208 | tf_op jit(solution)/shard_map/ppermute | solution.py:391
  99.9 1.3 %collective-permute-done.1.pieces_2_ = bf16[400,128]{1,0:T(8,128)(2,1)S(1)} collective-permute-done((bf16[400,128]{1,0:T(8,128)(2,1)S(1)}, bf16[400,128]{1,0:T(8,128)(2,1)S(1)}, u32[]{:S(2)}, u32[]{:S(2)}) %collective-permute-start.1) | collective-permute-done | bytes 102432 | tf_op jit(solution)/shard_map/ppermute | solution.py:391
  101.2 6.9 %collective-permute-done.2.pieces_3_ = bf16[400,128]{1,0:T(8,128)(2,1)S(1)} collective-permute-done((bf16[400,128]{1,0:T(8,128)(2,1)S(1)}, bf16[400,128]{1,0:T(8,128)(2,1)S(1)}, u32[]{:S(2)}, u32[]{:S(2)}) %collective-permute-start.2) | collective-permute-done | bytes 102432 | tf_op jit(solution)/shard_map/ppermute | solution.py:391
  108.0 0.8 shard_map.120
  108.8 0.8 shard_map.126
  109.6 1.2 %shard_map.124 = bf16[80,2880]{1,0:T(8,128)(2,1)} custom-call(s32[1]{0:T(128)} %bitcast.8.seat, bf16[32,24,128]{2,1,0:T(8,128)(2,1)S(1)} %all-to-all-done.2.refs_0_.near, bf16[32,24,128]{2,1,0:T(8,128)(2,1)S(1)} %collective-permute-done.4.refs_1_, bf16[32,24,128]{2,1,0:T(8,128)(2,1)S(1)} %collective-permute-done.5.refs_2_, ...), custom_call_target="tpu_custom_call" | custom-call | tf_op jit(solution)/shard_map/pallas_call | solution.py:427
  (23 shorter events, 0.8 us)
Async XLA Ops:
  2.4 12.6 %copy-start = (bf16[80,2880]{1,0:T(8,128)(2,1)S(1)}, bf16[80,2880]{1,0:T(8,128)(2,1)}, u32[]{:S(2)}) copy-start(bf16[80,2880]{1,0:T(8,128)(2,1)} %weight.1) | copy-start | bytes 1382404
  2.4 21.1 %all-to-all-start = ((bf16[4,400,128]{2,1,0:T(8,128)(2,1)}), bf16[4,400,128]{2,1,0:T(8,128)(2,1)S(1)}, u32[]{:S(2)}, u32[]{:S(2)}) async-start(bf16[4,400,128]{2,1,0:T(8,128)(2,1)} %pack.1), calls=%async_computation | async-start | bytes 819200 | tf_op jit(solution)/shard_map/all_to_all | solution.py:307
  13.4 0.7 copy-start.6
  15.4 0.8 copy-start.3
  15.4 0.8 copy-start.4
  15.4 0.8 copy-start.5
  25.0 7.5 %collective-permute-start.3 = (bf16[104,1536]{1,0:T(8,128)(2,1)S(1)}, bf16[104,1536]{1,0:T(8,128)(2,1)S(1)}, u32[]{:S(2)}, u32[]{:S(2)}) collective-permute-start(bf16[104,1536]{1,0:T(8,128)(2,1)S(1)} %get-tuple-element.32), channel_id=1, source_target_pairs={{0,4},{4,0},{1,5},{5,1},{2,6},{6,2},{3,7},{7,3},{8,12},{12,8},{9,1... | collective-permute-start | bytes 958472 | tf_op jit(solution)/shard_map/ppermute | solution.py:373
  33.5 24.6 %all-to-all-start.1 = ((bf16[64,24,128]{2,1,0:T(8,128)(2,1)}), bf16[64,24,128]{2,1,0:T(8,128)(2,1)S(1)}, u32[]{:S(2)}, u32[]{:S(2)}) async-start(bf16[64,24,128]{2,1,0:T(8,128)(2,1)} %shard_map.122), calls=%async_computation.1 | async-start | bytes 786432 | tf_op jit(solution)/shard_map/all_to_all | solution.py:307
  59.3 16.2 %all-to-all-start.2 = ((bf16[32,24,128]{2,1,0:T(8,128)(2,1)}), bf16[32,24,128]{2,1,0:T(8,128)(2,1)S(1)}, u32[]{:S(2)}, u32[]{:S(2)}) async-start(bf16[32,24,128]{2,1,0:T(8,128)(2,1)} %shard_map.123), calls=%async_computation.2 | async-start | bytes 393216 | tf_op jit(solution)/shard_map/all_to_all | solution.py:307
  67.2 30.4 %collective-permute-start = (bf16[400,128]{1,0:T(8,128)(2,1)S(1)}, bf16[400,128]{1,0:T(8,128)(2,1)S(1)}, u32[]{:S(2)}, u32[]{:S(2)}) collective-permute-start(bf16[400,128]{1,0:T(8,128)(2,1)S(1)} %get-tuple-element.25), channel_id=1, source_target_pairs={{0,1},{1,2},{2,3},{3,0},{4,5},{5,6},{6,7},{7,4},{8,9},{9,10},{10,1... | collective-permute-start | bytes 307208 | tf_op jit(solution)/shard_map/ppermute | solution.py:391
  75.6 34.0 %collective-permute-start.4 = (bf16[32,24,128]{2,1,0:T(8,128)(2,1)S(1)}, bf16[32,24,128]{2,1,0:T(8,128)(2,1)S(1)}, u32[]{:S(2)}, u32[]{:S(2)}) collective-permute-start(bf16[32,24,128]{2,1,0:T(8,128)(2,1)S(1)} %all-to-all-done.2.refs_0_.near), channel_id=1, source_target_pairs={{0,4},{4,0},{8,12},{12,8},{1,5},{5,1},{9,13},{13,9},{2,6},{6,2},{1... | collective-permute-start | bytes 589832 | tf_op jit(solution)/shard_map/ppermute | solution.py:421
  80.5 29.1 %collective-permute-start.5 = (bf16[32,24,128]{2,1,0:T(8,128)(2,1)S(1)}, bf16[32,24,128]{2,1,0:T(8,128)(2,1)S(1)}, u32[]{:S(2)}, u32[]{:S(2)}) collective-permute-start(bf16[32,24,128]{2,1,0:T(8,128)(2,1)S(1)} %all-to-all-done.2.refs_0_.near), channel_id=1, source_target_pairs={{0,8},{4,12},{8,0},{12,4},{1,9},{5,13},{9,1},{13,5},{2,10},{6,14},... | collective-permute-start | bytes 589832 | tf_op jit(solution)/shard_map/ppermute | solution.py:421
  82.7 26.9 %collective-permute-start.6 = (bf16[32,24,128]{2,1,0:T(8,128)(2,1)S(1)}, bf16[32,24,128]{2,1,0:T(8,128)(2,1)S(1)}, u32[]{:S(2)}, u32[]{:S(2)}) collective-permute-start(bf16[32,24,128]{2,1,0:T(8,128)(2,1)S(1)} %all-to-all-done.2.refs_0_.near), channel_id=1, source_target_pairs={{0,12},{4,8},{8,4},{12,0},{1,13},{5,9},{9,5},{13,1},{2,14},{6,10},... | collective-permute-start | bytes 589832 | tf_op jit(solution)/shard_map/ppermute | solution.py:421
  86.8 21.2 %copy-start.1 = (bf16[1,1,320,128]{3,2,1,0:T(8,128)(2,1)S(1)}, bf16[1,1,320,128]{3,2,1,0:T(8,128)(2,1)}, u32[]{:S(2)}) copy-start(bf16[1,1,320,128]{3,2,1,0:T(8,128)(2,1)} %param.7) | copy-start | bytes 245764
  86.8 21.2 %copy-start.2 = (bf16[1,1,320,128]{3,2,1,0:T(8,128)(2,1)S(1)}, bf16[1,1,320,128]{3,2,1,0:T(8,128)(2,1)}, u32[]{:S(2)}) copy-start(bf16[1,1,320,128]{3,2,1,0:T(8,128)(2,1)} %param.8) | copy-start | bytes 245764
  86.8 22.0 %all-to-all-start.3 = ((bf16[16,4,768]{2,1,0:T(4,128)(2,1)}), bf16[16,4,768]{2,1,0:T(4,128)(2,1)S(1)}, u32[]{:S(2)}, u32[]{:S(2)}) async-start(bf16[16,4,768]{2,1,0:T(4,128)(2,1)} %shard_map.125), calls=%async_computation.3 | async-start | bytes 196608 | tf_op jit(solution)/shard_map/all_to_all | solution.py:307
  90.5 10.7 %collective-permute-start.1 = (bf16[400,128]{1,0:T(8,128)(2,1)S(1)}, bf16[400,128]{1,0:T(8,128)(2,1)S(1)}, u32[]{:S(2)}, u32[]{:S(2)}) collective-permute-start(bf16[400,128]{1,0:T(8,128)(2,1)S(1)} %get-tuple-element.26), channel_id=1, source_target_pairs={{0,2},{1,3},{2,0},{3,1},{4,6},{5,7},{6,4},{7,5},{8,10},{9,11},{10,... | collective-permute-start | bytes 307208 | tf_op jit(solution)/shard_map/ppermute | solution.py:391
  97.7 10.3 %collective-permute-start.2 = (bf16[400,128]{1,0:T(8,128)(2,1)S(1)}, bf16[400,128]{1,0:T(8,128)(2,1)S(1)}, u32[]{:S(2)}, u32[]{:S(2)}) collective-permute-start(bf16[400,128]{1,0:T(8,128)(2,1)S(1)} %get-tuple-element.27), channel_id=1, source_target_pairs={{0,3},{1,0},{2,1},{3,2},{4,7},{5,4},{6,5},{7,6},{8,11},{9,8},{10,9... | collective-permute-start | bytes 307208 | tf_op jit(solution)/shard_map/ppermute | solution.py:391

commit v4 on v2

--- a/solution.py
+++ b/solution.py
@@ -109,7 +109,7 @@
         pieces[half] = terms[:, half * step : half * step + padded].astype(bf16)
 
 
-def gradient_body(core, gathered, pieces, kept, sent, cols, *, channels, step):
+def gradient_body(core, gathered, pieces, target, cols, *, channels, step, other):
     rows = gathered.shape[0]
     quarter = gathered.shape[1] - channels
     fill(cols, rows, functools.partial(activated, gathered, channels), 1)
@@ -117,12 +117,11 @@
     if cols.shape[0] > whole:
         cols[whole:, :] = jnp.zeros((cols.shape[0] - whole, cols.shape[1]), bf16)
     upstream = jnp.concatenate([gathered[h, channels:, :] for h in range(rows)], axis=1)
-    padded = kept.shape[1]
-    for target, half in ((sent, 1 - core[0]), (kept, core[0])):
-        start = pl.multiple_of(half * step, 8)
-        product = dot(upstream, cols[pl.ds(start, padded), :], 1, 1)
-        target[:quarter, :] = product.astype(bf16)
-        target[quarter:, :] = pieces[half]
+    half = 1 - core[0] if other else core[0]
+    start = pl.multiple_of(half * step, 8)
+    product = dot(upstream, cols[pl.ds(start, target.shape[1]), :], 1, 1)
+    target[:quarter, :] = product.astype(bf16)
+    target[quarter:, :] = pieces[half]
 
 
 def convolution_body(
@@ -248,23 +247,24 @@
         message[target] = turned[first : first + capacity].astype(bf16)
 
 
-def finish_body(
-    core, near, far, owned, master, first_moment, second_moment, filled,
-    new_weight, new_master, new_first, new_second, *, step, strips, root,
-):
-    quarter, capacity = new_weight.shape[0], master.shape[0]
+def collect_weight_body(core, near, far, new_weight, *, step):
     ours, others = flat(near), flat(far)
     first = core[0] == 0
     rows = [jnp.where(first, ours, others)[:step], jnp.where(first, others, ours)[:step]]
     rows = jnp.concatenate(rows, axis=0).astype(bf16)
-    turned = dot(unit(quarter, 0), rows, 1, 1)
-    new_weight[...] = turned.astype(bf16)
+    new_weight[...] = dot(unit(new_weight.shape[0], 0), rows, 1, 1).astype(bf16)
+
+
+def finish_body(
+    owned, master, first_moment, second_moment, filled,
+    new_master, new_first, new_second, *, step, strips, root,
+):
     halves = []
     for half in range(owned.shape[0] // strips):
         total = owned[half * strips].astype(f32)
         for strip in range(1, strips):
             total = total + owned[half * strips + strip].astype(f32)
-        halves.append(total[:capacity, :step])
+        halves.append(total[:, :step])
     grads = jnp.concatenate(halves, axis=1) / root
     fresh, first_new, second_new = adam(
         grads, master[...], first_moment[...], second_moment[...]
@@ -338,13 +338,16 @@
         (gathered, slots, filled, turned, pieces)
     )
 
-    kept, sent = call(
-        functools.partial(gradient_body, channels=channels, step=step),
-        [jax.ShapeDtypeStruct((quarter + height, padded), bf16)] * 2,
-        [pltpu.VMEM(((cores - 1) * step + padded, rows * width), bf16)],
-        scalars=1,
-        inputs=2,
-    )(core_scalar, gathered, pieces)
+    sent, kept = (
+        call(
+            functools.partial(gradient_body, channels=channels, step=step, other=other),
+            jax.ShapeDtypeStruct((quarter + height, padded), bf16),
+            [pltpu.VMEM(((cores - 1) * step + padded, rows * width), bf16)],
+            scalars=1,
+            inputs=2,
+        )(core_scalar, gathered, pieces)
+        for other in (True, False)
+    )
     swapped = lax.ppermute(sent, "core", swap)
 
     residual = lax.dynamic_slice_in_dim(gathered, strip * quarter, quarter, axis=1)
@@ -393,13 +396,17 @@
         jax.ShapeDtypeStruct((cores * strips, capacity, padded), bf16),
     )(near)
     owned_rows = exchange(owned_rows, ("core", "strip"))
-    new_weight, new_master, new_first, new_second = call(
+    new_weight = call(
+        functools.partial(collect_weight_body, step=step),
+        jax.ShapeDtypeStruct((quarter, taken), bf16),
+        scalars=1,
+        inputs=2,
+    )(core_scalar, near, far)
+    owned_rows, new_weight = lax.optimization_barrier((owned_rows, new_weight))
+    new_master, new_first, new_second = call(
         functools.partial(finish_body, step=step, strips=strips, root=root),
-        [jax.ShapeDtypeStruct((quarter, taken), bf16)]
-        + [jax.ShapeDtypeStruct(master.shape, f32)] * 3,
-        scalars=1,
-        inputs=7,
-    )(core_scalar, near, far, owned_rows, master, first_moment, second_moment, filled)
+        [jax.ShapeDtypeStruct(master.shape, f32)] * 3,
+    )(owned_rows, master, first_moment, second_moment, filled)
     return (output[None, None], grad_input[None, None], new_weight, new_master, new_first, new_second)
 
 

time: 112 us -> 112 us (level)
  Pallas kernels: 9.07 us -> 10.4 us
    pallas_call x1 -> x3, Pallas kernels: 1.55 us -> 3.3 us  [the longest x2 2.14 us: local(): call(functools.partial(gradient_body, channels=channels, step=step, other...]
  transfers between devices with their start and end apart: 8 -> 8, of which waited for: 5 -> 5; matrix products, arithmetic and copies ran while one was open for 2% -> 2% of each run, Pallas kernels for 3% -> 5%
where the time goes in v4:
time: 112 us; the launch traced here: 111 us
  starting transfers between devices  52.3 us (47%)
  waiting for transfers between devices  25.3 us (23%)
  blocking collectives  19 us (17%)
  Pallas kernels  10.4 us (9%)
  local copies, waits for them, and re-layouts  2.21 us (2%)
  other arithmetic  1.51 us (1%)
    all_to_all x3, starting transfers between devices, exchange(): return lax.all_to_all(value, axes, 0, 0, tiled=True)  25.7 us
    all_to_all x3, waiting for transfers between devices, exchange(): return lax.all_to_all(value, axes, 0, 0, tiled=True)  19.7 us
    all_to_all x1, blocking collectives, exchange(): return lax.all_to_all(value, axes, 0, 0, tiled=True)  19 us
    ppermute x3, starting transfers between devices, local(): returned.append(lax.ppermute(results[ahead], 'strip', pairs))  14.5 us
    ppermute x1, starting transfers between devices, local(): swapped = lax.ppermute(sent, 'core', swap)  6.29 us
    ppermute x1, starting transfers between devices, local(): far = lax.ppermute(near, 'core', swap)  5.76 us
    ppermute x3, waiting for transfers between devices, local(): returned.append(lax.ppermute(results[ahead], 'strip', pairs))  5.42 us
  transfers between devices with their start and end apart: 8, of which 5 were waited for; matrix products, arithmetic and copies ran while one was open for 2% of the time, Pallas kernels for 5%

profile of v4, /device:TPU:1, one launch (start us, length us, event | category | flops | bytes accessed | tf_op | source)
XLA Modules:
  0.0 111.5 jit_solution(13916885310937507248)
XLA Ops:
  0.6 1.7 %pack.1 = bf16[4,400,128]{2,1,0:T(8,128)(2,1)} custom-call(bf16[320,128]{1,0:T(8,128)(2,1)} %bitcast.10, bf16[320,128]{1,0:T(8,128)(2,1)} %bitcast.12), custom_call_target="tpu_custom_call" | custom-call | tf_op jit(solution)/shard_map/pack/pallas_call | solution.py:311
  2.4 11.0 %all-to-all-start = ((bf16[4,400,128]{2,1,0:T(8,128)(2,1)}), bf16[4,400,128]{2,1,0:T(8,128)(2,1)S(1)}, u32[]{:S(2)}, u32[]{:S(2)}) async-start(bf16[4,400,128]{2,1,0:T(8,128)(2,1)} %pack.1), calls=%async_computation | async-start | bytes 819200 | tf_op jit(solution)/shard_map/all_to_all | solution.py:287
  13.4 0.7 copy-done.6
  14.1 0.2 convert_reduce_fusion
  14.3 0.6 convert_reduce_fusion.1
  15.0 0.4 copy.17
  15.4 0.4 copy.18
  15.8 0.4 copy-done.3
  16.3 0.7 fusion.1.filled
  17.0 6.5 %all-to-all-done.gathered = bf16[4,400,128]{2,1,0:T(8,128)(2,1)S(1)} async-done(((bf16[4,400,128]{2,1,0:T(8,128)(2,1)}), bf16[4,400,128]{2,1,0:T(8,128)(2,1)S(1)}, u32[]{:S(2)}, u32[]{:S(2)}) %all-to-all-start) | async-done | bytes 409632 | tf_op jit(solution)/shard_map/all_to_all | solution.py:287
  23.5 1.1 shard_map.122
  24.6 6.3 %collective-permute-start.3 = (bf16[104,1536]{1,0:T(8,128)(2,1)S(1)}, bf16[104,1536]{1,0:T(8,128)(2,1)S(1)}, u32[]{:S(2)}, u32[]{:S(2)}) collective-permute-start(bf16[104,1536]{1,0:T(8,128)(2,1)S(1)} %shard_map.122), channel_id=1, source_target_pairs={{0,4},{4,0},{1,5},{5,1},{2,6},{6,2},{3,7},{7,3},{8,12},{12,8},{9,1... | collective-permute-start | bytes 958472 | tf_op jit(solution)/shard_map/ppermute | solution.py:351
  30.9 1.1 shard_map.121.kept
  31.9 0.1 collective-permute-done.3.received
  32.1 0.9 shard_map.123
  33.0 11.4 %all-to-all-start.1 = ((bf16[64,24,128]{2,1,0:T(8,128)(2,1)}), bf16[64,24,128]{2,1,0:T(8,128)(2,1)S(1)}, u32[]{:S(2)}, u32[]{:S(2)}) async-start(bf16[64,24,128]{2,1,0:T(8,128)(2,1)} %shard_map.123), calls=%async_computation.1 | async-start | bytes 786432 | tf_op jit(solution)/shard_map/all_to_all | solution.py:287
  44.4 13.2 %all-to-all-done.1.received = bf16[64,24,128]{2,1,0:T(8,128)(2,1)S(1)} async-done(((bf16[64,24,128]{2,1,0:T(8,128)(2,1)}), bf16[64,24,128]{2,1,0:T(8,128)(2,1)S(1)}, u32[]{:S(2)}, u32[]{:S(2)}) %all-to-all-start.1) | async-done | bytes 393248 | tf_op jit(solution)/shard_map/all_to_all | solution.py:287
  57.6 0.6 shard_map.124
  58.3 19.0 %all_to_all.20.near = bf16[64,24,128]{2,1,0:T(8,128)(2,1)S(1)} all-to-all(bf16[64,24,128]{2,1,0:T(8,128)(2,1)S(1)} %shard_map.124), channel_id=1, replica_groups=mesh['line'=8,'group'=8,'core'=2,'strip'=4] {'line','group'}, dimensions={0} | all-to-all | bytes 786432 | tf_op jit(solution)/shard_map/all_to_all | solution.py:287
  77.2 5.8 %collective-permute-start.4 = (bf16[64,24,128]{2,1,0:T(8,128)(2,1)S(1)}, bf16[64,24,128]{2,1,0:T(8,128)(2,1)S(1)}, u32[]{:S(2)}, u32[]{:S(2)}) collective-permute-start(bf16[64,24,128]{2,1,0:T(8,128)(2,1)S(1)} %all_to_all.20.near), channel_id=1, source_target_pairs={{0,4},{4,0},{1,5},{5,1},{2,6},{6,2},{3,7},{7,3},{8,12},{12,8},{9,1... | collective-permute-start | bytes 1179656 | tf_op jit(solution)/shard_map/ppermute | solution.py:393
  83.0 0.2 copy.19.turned
  83.2 0.9 shard_map.125
  84.1 3.3 %all-to-all-start.3 = ((bf16[8,4,1536]{2,1,0:T(4,128)(2,1)}), bf16[8,4,1536]{2,1,0:T(4,128)(2,1)S(1)}, u32[]{:S(2)}, u32[]{:S(2)}) async-start(bf16[8,4,1536]{2,1,0:T(4,128)(2,1)} %shard_map.125), calls=%async_computation.3 | async-start | bytes 196608 | tf_op jit(solution)/shard_map/all_to_all | solution.py:287
  87.4 1.3 %shard_map.119 = (bf16[400,128]{1,0:T(8,128)(2,1)S(1)}, bf16[400,128]{1,0:T(8,128)(2,1)S(1)}, bf16[400,128]{1,0:T(8,128)(2,1)S(1)}, bf16[400,128]{1,0:T(8,128)(2,1)S(1)}) custom-call(s32[1]{0:T(128)} %bitcast.strip, bf16[4,400,128]{2,1,0:T(8,128)(2,1)S(1)} %all-to-all-done.gathered, bf16[4,80,128]{2,1,0:T(8,128)(2,1)S(1)} %constant_dynamic-slice_fusion.residual, ...), custom_call_target="tpu_custom_call" | custom-call | tf_op jit(solution)/shard_map/pallas_call | solution.py:354
  88.8 4.1 %collective-permute-start = (bf16[400,128]{1,0:T(8,128)(2,1)S(1)}, bf16[400,128]{1,0:T(8,128)(2,1)S(1)}, u32[]{:S(2)}, u32[]{:S(2)}) collective-permute-start(bf16[400,128]{1,0:T(8,128)(2,1)S(1)} %get-tuple-element.25), channel_id=1, source_target_pairs={{0,1},{1,2},{2,3},{3,0},{4,5},{5,6},{6,7},{7,4},{8,9},{9,10},{10,1... | collective-permute-start | bytes 307208 | tf_op jit(solution)/shard_map/ppermute | solution.py:369
  92.9 5.2 %collective-permute-start.1 = (bf16[400,128]{1,0:T(8,128)(2,1)S(1)}, bf16[400,128]{1,0:T(8,128)(2,1)S(1)}, u32[]{:S(2)}, u32[]{:S(2)}) collective-permute-start(bf16[400,128]{1,0:T(8,128)(2,1)S(1)} %get-tuple-element.26), channel_id=1, source_target_pairs={{0,2},{1,3},{2,0},{3,1},{4,6},{5,7},{6,4},{7,5},{8,10},{9,11},{10,... | collective-permute-start | bytes 307208 | tf_op jit(solution)/shard_map/ppermute | solution.py:369
  98.1 5.2 %collective-permute-start.2 = (bf16[400,128]{1,0:T(8,128)(2,1)S(1)}, bf16[400,128]{1,0:T(8,128)(2,1)S(1)}, u32[]{:S(2)}, u32[]{:S(2)}) collective-permute-start(bf16[400,128]{1,0:T(8,128)(2,1)S(1)} %get-tuple-element.27), channel_id=1, source_target_pairs={{0,3},{1,0},{2,1},{3,2},{4,7},{5,4},{6,5},{7,6},{8,11},{9,8},{10,9... | collective-permute-start | bytes 307208 | tf_op jit(solution)/shard_map/ppermute | solution.py:369
  103.3 2.2 %collective-permute-done.1.pieces_2_ = bf16[400,128]{1,0:T(8,128)(2,1)S(1)} collective-permute-done((bf16[400,128]{1,0:T(8,128)(2,1)S(1)}, bf16[400,128]{1,0:T(8,128)(2,1)S(1)}, u32[]{:S(2)}, u32[]{:S(2)}) %collective-permute-start.1) | collective-permute-done | bytes 102432 | tf_op jit(solution)/shard_map/ppermute | solution.py:369
  105.6 3.2 %collective-permute-done.2.pieces_3_ = bf16[400,128]{1,0:T(8,128)(2,1)S(1)} collective-permute-done((bf16[400,128]{1,0:T(8,128)(2,1)S(1)}, bf16[400,128]{1,0:T(8,128)(2,1)S(1)}, u32[]{:S(2)}, u32[]{:S(2)}) %collective-permute-start.2) | collective-permute-done | bytes 102432 | tf_op jit(solution)/shard_map/ppermute | solution.py:369
  108.8 0.8 shard_map.120
  109.5 1.2 %shard_map.126 = bf16[80,2880]{1,0:T(8,128)(2,1)} custom-call(s32[1]{0:T(128)} %bitcast.8.core, bf16[64,24,128]{2,1,0:T(8,128)(2,1)S(1)} %all_to_all.20.near, bf16[64,24,128]{2,1,0:T(8,128)(2,1)S(1)} %collective-permute-done.4.far), custom_call_target="tpu_custom_call" | custom-call | tf_op jit(solution)/shard_map/pallas_call | solution.py:399
  110.7 0.8 shard_map.127
  (19 shorter events, 0.3 us)
Async XLA Ops:
  2.4 12.6 %copy-start = (bf16[80,2880]{1,0:T(8,128)(2,1)S(1)}, bf16[80,2880]{1,0:T(8,128)(2,1)}, u32[]{:S(2)}) copy-start(bf16[80,2880]{1,0:T(8,128)(2,1)} %weight.1) | copy-start | bytes 1382404
  2.4 21.1 %all-to-all-start = ((bf16[4,400,128]{2,1,0:T(8,128)(2,1)}), bf16[4,400,128]{2,1,0:T(8,128)(2,1)S(1)}, u32[]{:S(2)}, u32[]{:S(2)}) async-start(bf16[4,400,128]{2,1,0:T(8,128)(2,1)} %pack.1), calls=%async_computation | async-start | bytes 819200 | tf_op jit(solution)/shard_map/all_to_all | solution.py:287
  13.4 0.7 copy-start.6
  15.4 0.8 copy-start.3
  15.4 0.8 copy-start.4
  15.4 0.8 copy-start.5
  24.6 7.5 %collective-permute-start.3 = (bf16[104,1536]{1,0:T(8,128)(2,1)S(1)}, bf16[104,1536]{1,0:T(8,128)(2,1)S(1)}, u32[]{:S(2)}, u32[]{:S(2)}) collective-permute-start(bf16[104,1536]{1,0:T(8,128)(2,1)S(1)} %shard_map.122), channel_id=1, source_target_pairs={{0,4},{4,0},{1,5},{5,1},{2,6},{6,2},{3,7},{7,3},{8,12},{12,8},{9,1... | collective-permute-start | bytes 958472 | tf_op jit(solution)/shard_map/ppermute | solution.py:351
  33.0 24.6 %all-to-all-start.1 = ((bf16[64,24,128]{2,1,0:T(8,128)(2,1)}), bf16[64,24,128]{2,1,0:T(8,128)(2,1)S(1)}, u32[]{:S(2)}, u32[]{:S(2)}) async-start(bf16[64,24,128]{2,1,0:T(8,128)(2,1)} %shard_map.123), calls=%async_computation.1 | async-start | bytes 786432 | tf_op jit(solution)/shard_map/all_to_all | solution.py:287
  77.2 32.3 %collective-permute-start.4 = (bf16[64,24,128]{2,1,0:T(8,128)(2,1)S(1)}, bf16[64,24,128]{2,1,0:T(8,128)(2,1)S(1)}, u32[]{:S(2)}, u32[]{:S(2)}) collective-permute-start(bf16[64,24,128]{2,1,0:T(8,128)(2,1)S(1)} %all_to_all.20.near), channel_id=1, source_target_pairs={{0,4},{4,0},{1,5},{5,1},{2,6},{6,2},{3,7},{7,3},{8,12},{12,8},{9,1... | collective-permute-start | bytes 1179656 | tf_op jit(solution)/shard_map/ppermute | solution.py:393
  84.1 26.6 %all-to-all-start.3 = ((bf16[8,4,1536]{2,1,0:T(4,128)(2,1)}), bf16[8,4,1536]{2,1,0:T(4,128)(2,1)S(1)}, u32[]{:S(2)}, u32[]{:S(2)}) async-start(bf16[8,4,1536]{2,1,0:T(4,128)(2,1)} %shard_map.125), calls=%async_computation.3 | async-start | bytes 196608 | tf_op jit(solution)/shard_map/all_to_all | solution.py:287
  87.4 21.3 %copy-start.1 = (bf16[1,1,320,128]{3,2,1,0:T(8,128)(2,1)S(1)}, bf16[1,1,320,128]{3,2,1,0:T(8,128)(2,1)}, u32[]{:S(2)}) copy-start(bf16[1,1,320,128]{3,2,1,0:T(8,128)(2,1)} %param.7) | copy-start | bytes 245764
  87.4 21.3 %copy-start.2 = (bf16[1,1,320,128]{3,2,1,0:T(8,128)(2,1)S(1)}, bf16[1,1,320,128]{3,2,1,0:T(8,128)(2,1)}, u32[]{:S(2)}) copy-start(bf16[1,1,320,128]{3,2,1,0:T(8,128)(2,1)} %param.8) | copy-start | bytes 245764
  88.8 14.6 %collective-permute-start = (bf16[400,128]{1,0:T(8,128)(2,1)S(1)}, bf16[400,128]{1,0:T(8,128)(2,1)S(1)}, u32[]{:S(2)}, u32[]{:S(2)}) collective-permute-start(bf16[400,128]{1,0:T(8,128)(2,1)S(1)} %get-tuple-element.25), channel_id=1, source_target_pairs={{0,1},{1,2},{2,3},{3,0},{4,5},{5,6},{6,7},{7,4},{8,9},{9,10},{10,1... | collective-permute-start | bytes 307208 | tf_op jit(solution)/shard_map/ppermute | solution.py:369
  92.9 12.7 %collective-permute-start.1 = (bf16[400,128]{1,0:T(8,128)(2,1)S(1)}, bf16[400,128]{1,0:T(8,128)(2,1)S(1)}, u32[]{:S(2)}, u32[]{:S(2)}) collective-permute-start(bf16[400,128]{1,0:T(8,128)(2,1)S(1)} %get-tuple-element.26), channel_id=1, source_target_pairs={{0,2},{1,3},{2,0},{3,1},{4,6},{5,7},{6,4},{7,5},{8,10},{9,11},{10,... | collective-permute-start | bytes 307208 | tf_op jit(solution)/shard_map/ppermute | solution.py:369
  98.1 10.6 %collective-permute-start.2 = (bf16[400,128]{1,0:T(8,128)(2,1)S(1)}, bf16[400,128]{1,0:T(8,128)(2,1)S(1)}, u32[]{:S(2)}, u32[]{:S(2)}) collective-permute-start(bf16[400,128]{1,0:T(8,128)(2,1)S(1)} %get-tuple-element.27), channel_id=1, source_target_pairs={{0,3},{1,0},{2,1},{3,2},{4,7},{5,4},{6,5},{7,6},{8,11},{9,8},{10,9... | collective-permute-start | bytes 307208 | tf_op jit(solution)/shard_map/ppermute | solution.py:369

commit v5 on v4

--- a/solution.py
+++ b/solution.py
@@ -183,7 +183,7 @@
     return master - update, first_new, second_new
 
 
-def publish_body(strip, received, slots, message, *, quarter, capacity, cores, root):
+def publish_body(strip, received, slots, message, *, quarter, capacity, groups, cores, root):
     chips, chunk, _ = received.shape
     strips = slots.shape[0]
     columns = max(LANES, chips * cores * capacity)
@@ -192,6 +192,8 @@
         mine = jnp.where(strip[0] == other, slots[other : other + 1, :], mine)
     wide = jnp.concatenate([mine] * 3, axis=1)
     owner, place = wide // capacity, wide % capacity
+    lines = chips // groups
+    source = owner // cores % groups * lines + owner // (cores * groups)
     share = TERMS * 3 * capacity
     row = lax.broadcasted_iota(jnp.int32, (LANES, 3 * LANES), 0) - quarter
     array = lax.broadcasted_iota(jnp.int32, (LANES, 3 * LANES), 1) // LANES
@@ -206,9 +208,7 @@
     picked = dot(jnp.concatenate(values, axis=0).astype(bf16), here, 1, 0)
     state = jnp.zeros((chunk, 3 * LANES), f32)
     for chip in range(chips):
-        state = jnp.where(
-            owner // cores == chip, picked[chip * chunk : (chip + 1) * chunk], state
-        )
+        state = jnp.where(source == chip, picked[chip * chunk : (chip + 1) * chunk], state)
     fresh, _, _ = adam(
         grads / root, state[:, :LANES], state[:, LANES : 2 * LANES], state[:, 2 * LANES :]
     )
@@ -219,8 +219,9 @@
     span = cores * capacity
     per_tile = LANES // span
     for chip in range(chips):
-        tile = chosen[:, chip // per_tile * LANES : (chip // per_tile + 1) * LANES]
-        shift = (quarter - span * (chip % per_tile)) % LANES
+        number = chip % lines * groups + chip // lines
+        tile = chosen[:, number // per_tile * LANES : (number // per_tile + 1) * LANES]
+        shift = (quarter - span * (number % per_tile)) % LANES
         moved = tile if shift == 0 else pltpu.roll(tile, shift, 1)
         value = jnp.where(lane < quarter, fresh, jnp.where(lane < quarter + span, moved, 0.0))
         message[chip] = value.astype(bf16)
@@ -374,14 +375,17 @@
         scalars=1,
         inputs=2,
     )(core_scalar, kept, swapped)
-    by_chip = exchange(by_chip, ("line", "group"))
+    by_chip = exchange(by_chip, ("group", "line"))
     message = call(
-        functools.partial(publish_body, quarter=quarter, capacity=capacity, cores=cores, root=root),
+        functools.partial(
+            publish_body, quarter=quarter, capacity=capacity, groups=groups, cores=cores,
+            root=root,
+        ),
         jax.ShapeDtypeStruct((chips, chunk, LANES), bf16),
         scalars=1,
         inputs=2,
     )(strip_scalar, by_chip, slots)
-    near = exchange(message, ("line", "group"))
+    near = exchange(message, ("group", "line"))
 
     output, grad_input = call(
         functools.partial(collect_body, quarter=quarter),

time: 112 us -> 112 us (level)
  no operation moved by 1% of the time
where the time goes in v5:
time: 112 us
  starting transfers between devices  52.4 us (47%)
  waiting for transfers between devices  25.5 us (23%)
  blocking collectives  18.8 us (17%)
  Pallas kernels  10.4 us (9%)
  local copies, waits for them, and re-layouts  2.21 us (2%)
  other arithmetic  1.51 us (1%)
    all_to_all x3, starting transfers between devices, exchange(): return lax.all_to_all(value, axes, 0, 0, tiled=True)  25.7 us
    all_to_all x3, waiting for transfers between devices, exchange(): return lax.all_to_all(value, axes, 0, 0, tiled=True)  20.7 us
    all_to_all x1, blocking collectives, exchange(): return lax.all_to_all(value, axes, 0, 0, tiled=True)  18.8 us
    ppermute x3, starting transfers between devices, local(): returned.append(lax.ppermute(results[ahead], 'strip', pairs))  14.5 us
    ppermute x1, starting transfers between devices, local(): swapped = lax.ppermute(sent, 'core', swap)  6.29 us
    ppermute x1, starting transfers between devices, local(): far = lax.ppermute(near, 'core', swap)  5.94 us
    ppermute x3, waiting for transfers between devices, local(): returned.append(lax.ppermute(results[ahead], 'strip', pairs))  4.64 us
  transfers between devices with their start and end apart: 8, of which 5 were waited for; matrix products, arithmetic and copies ran while one was open for 2% of the time, Pallas kernels for 5%

profile of v5, /device:TPU:1, one launch (start us, length us, event | category | flops | bytes accessed | tf_op | source)
XLA Modules:
  0.0 111.7 jit_solution(2981717049061816180)
XLA Ops:
  0.6 1.7 %pack.1 = bf16[4,400,128]{2,1,0:T(8,128)(2,1)} custom-call(bf16[320,128]{1,0:T(8,128)(2,1)} %bitcast.10, bf16[320,128]{1,0:T(8,128)(2,1)} %bitcast.12), custom_call_target="tpu_custom_call" | custom-call | tf_op jit(solution)/shard_map/pack/pallas_call | solution.py:312
  2.4 11.0 %all-to-all-start = ((bf16[4,400,128]{2,1,0:T(8,128)(2,1)}), bf16[4,400,128]{2,1,0:T(8,128)(2,1)S(1)}, u32[]{:S(2)}, u32[]{:S(2)}) async-start(bf16[4,400,128]{2,1,0:T(8,128)(2,1)} %pack.1), calls=%async_computation | async-start | bytes 819200 | tf_op jit(solution)/shard_map/all_to_all | solution.py:288
  13.4 0.7 copy-done.6
  14.1 0.2 convert_reduce_fusion
  14.3 0.6 convert_reduce_fusion.1
  15.0 0.4 copy.17
  15.4 0.4 copy.18
  15.8 0.4 copy-done.3
  16.2 0.1 shard_map.118.pieces
  16.3 0.7 fusion.1.filled
  17.0 6.5 %all-to-all-done.gathered = bf16[4,400,128]{2,1,0:T(8,128)(2,1)S(1)} async-done(((bf16[4,400,128]{2,1,0:T(8,128)(2,1)}), bf16[4,400,128]{2,1,0:T(8,128)(2,1)S(1)}, u32[]{:S(2)}, u32[]{:S(2)}) %all-to-all-start) | async-done | bytes 409632 | tf_op jit(solution)/shard_map/all_to_all | solution.py:288
  23.5 1.1 shard_map.122
  24.6 6.3 %collective-permute-start.3 = (bf16[104,1536]{1,0:T(8,128)(2,1)S(1)}, bf16[104,1536]{1,0:T(8,128)(2,1)S(1)}, u32[]{:S(2)}, u32[]{:S(2)}) collective-permute-start(bf16[104,1536]{1,0:T(8,128)(2,1)S(1)} %shard_map.122), channel_id=1, source_target_pairs={{0,4},{4,0},{1,5},{5,1},{2,6},{6,2},{3,7},{7,3},{8,12},{12,8},{9,1... | collective-permute-start | bytes 958472 | tf_op jit(solution)/shard_map/ppermute | solution.py:352
  30.9 1.1 shard_map.121.kept
  31.9 0.1 collective-permute-done.3.received
  32.1 0.9 shard_map.123
  33.0 11.4 %all-to-all-start.1 = ((bf16[64,24,128]{2,1,0:T(8,128)(2,1)}), bf16[64,24,128]{2,1,0:T(8,128)(2,1)S(1)}, u32[]{:S(2)}, u32[]{:S(2)}) async-start(bf16[64,24,128]{2,1,0:T(8,128)(2,1)} %shard_map.123), calls=%async_computation.1 | async-start | bytes 786432 | tf_op jit(solution)/shard_map/all_to_all | solution.py:288
  44.4 14.2 %all-to-all-done.1.received = bf16[64,24,128]{2,1,0:T(8,128)(2,1)S(1)} async-done(((bf16[64,24,128]{2,1,0:T(8,128)(2,1)}), bf16[64,24,128]{2,1,0:T(8,128)(2,1)S(1)}, u32[]{:S(2)}, u32[]{:S(2)}) %all-to-all-start.1) | async-done | bytes 393248 | tf_op jit(solution)/shard_map/all_to_all | solution.py:288
  58.6 0.6 shard_map.124
  59.2 18.8 %all_to_all.20.near = bf16[64,24,128]{2,1,0:T(8,128)(2,1)S(1)} all-to-all(bf16[64,24,128]{2,1,0:T(8,128)(2,1)S(1)} %shard_map.124), channel_id=1, replica_groups=mesh['line'=8,'group'=8,'core'=2,'strip'=4] {'group','line'}, dimensions={0} | all-to-all | bytes 786432 | tf_op jit(solution)/shard_map/all_to_all | solution.py:288
  78.0 5.9 %collective-permute-start.4 = (bf16[64,24,128]{2,1,0:T(8,128)(2,1)S(1)}, bf16[64,24,128]{2,1,0:T(8,128)(2,1)S(1)}, u32[]{:S(2)}, u32[]{:S(2)}) collective-permute-start(bf16[64,24,128]{2,1,0:T(8,128)(2,1)S(1)} %all_to_all.20.near), channel_id=1, source_target_pairs={{0,4},{4,0},{1,5},{5,1},{2,6},{6,2},{3,7},{7,3},{8,12},{12,8},{9,1... | collective-permute-start | bytes 1179656 | tf_op jit(solution)/shard_map/ppermute | solution.py:397
  84.0 0.2 copy.19.turned
  84.2 0.9 shard_map.125
  85.1 3.3 %all-to-all-start.3 = ((bf16[8,4,1536]{2,1,0:T(4,128)(2,1)}), bf16[8,4,1536]{2,1,0:T(4,128)(2,1)S(1)}, u32[]{:S(2)}, u32[]{:S(2)}) async-start(bf16[8,4,1536]{2,1,0:T(4,128)(2,1)} %shard_map.125), calls=%async_computation.3 | async-start | bytes 196608 | tf_op jit(solution)/shard_map/all_to_all | solution.py:288
  88.4 1.3 %shard_map.119 = (bf16[400,128]{1,0:T(8,128)(2,1)S(1)}, bf16[400,128]{1,0:T(8,128)(2,1)S(1)}, bf16[400,128]{1,0:T(8,128)(2,1)S(1)}, bf16[400,128]{1,0:T(8,128)(2,1)S(1)}) custom-call(s32[1]{0:T(128)} %bitcast.strip, bf16[4,400,128]{2,1,0:T(8,128)(2,1)S(1)} %all-to-all-done.gathered, bf16[4,80,128]{2,1,0:T(8,128)(2,1)S(1)} %constant_dynamic-slice_fusion.residual, ...), custom_call_target="tpu_custom_call" | custom-call | tf_op jit(solution)/shard_map/pallas_call | solution.py:355
  89.7 4.1 %collective-permute-start = (bf16[400,128]{1,0:T(8,128)(2,1)S(1)}, bf16[400,128]{1,0:T(8,128)(2,1)S(1)}, u32[]{:S(2)}, u32[]{:S(2)}) collective-permute-start(bf16[400,128]{1,0:T(8,128)(2,1)S(1)} %get-tuple-element.25), channel_id=1, source_target_pairs={{0,1},{1,2},{2,3},{3,0},{4,5},{5,6},{6,7},{7,4},{8,9},{9,10},{10,1... | collective-permute-start | bytes 307208 | tf_op jit(solution)/shard_map/ppermute | solution.py:370
  93.9 5.2 %collective-permute-start.1 = (bf16[400,128]{1,0:T(8,128)(2,1)S(1)}, bf16[400,128]{1,0:T(8,128)(2,1)S(1)}, u32[]{:S(2)}, u32[]{:S(2)}) collective-permute-start(bf16[400,128]{1,0:T(8,128)(2,1)S(1)} %get-tuple-element.26), channel_id=1, source_target_pairs={{0,2},{1,3},{2,0},{3,1},{4,6},{5,7},{6,4},{7,5},{8,10},{9,11},{10,... | collective-permute-start | bytes 307208 | tf_op jit(solution)/shard_map/ppermute | solution.py:370
  99.1 5.2 %collective-permute-start.2 = (bf16[400,128]{1,0:T(8,128)(2,1)S(1)}, bf16[400,128]{1,0:T(8,128)(2,1)S(1)}, u32[]{:S(2)}, u32[]{:S(2)}) collective-permute-start(bf16[400,128]{1,0:T(8,128)(2,1)S(1)} %get-tuple-element.27), channel_id=1, source_target_pairs={{0,3},{1,0},{2,1},{3,2},{4,7},{5,4},{6,5},{7,6},{8,11},{9,8},{10,9... | collective-permute-start | bytes 307208 | tf_op jit(solution)/shard_map/ppermute | solution.py:370
  104.4 4.6 %collective-permute-done.2.pieces_3_ = bf16[400,128]{1,0:T(8,128)(2,1)S(1)} collective-permute-done((bf16[400,128]{1,0:T(8,128)(2,1)S(1)}, bf16[400,128]{1,0:T(8,128)(2,1)S(1)}, u32[]{:S(2)}, u32[]{:S(2)}) %collective-permute-start.2) | collective-permute-done | bytes 102432 | tf_op jit(solution)/shard_map/ppermute | solution.py:370
  109.0 0.8 shard_map.120
  109.7 1.2 %shard_map.126 = bf16[80,2880]{1,0:T(8,128)(2,1)} custom-call(s32[1]{0:T(128)} %bitcast.8.core, bf16[64,24,128]{2,1,0:T(8,128)(2,1)S(1)} %all_to_all.20.near, bf16[64,24,128]{2,1,0:T(8,128)(2,1)S(1)} %collective-permute-done.4.far), custom_call_target="tpu_custom_call" | custom-call | tf_op jit(solution)/shard_map/pallas_call | solution.py:403
  110.9 0.8 shard_map.127
  (19 shorter events, 0.3 us)
Async XLA Ops:
  2.4 12.6 %copy-start = (bf16[80,2880]{1,0:T(8,128)(2,1)S(1)}, bf16[80,2880]{1,0:T(8,128)(2,1)}, u32[]{:S(2)}) copy-start(bf16[80,2880]{1,0:T(8,128)(2,1)} %weight.1) | copy-start | bytes 1382404
  2.4 21.1 %all-to-all-start = ((bf16[4,400,128]{2,1,0:T(8,128)(2,1)}), bf16[4,400,128]{2,1,0:T(8,128)(2,1)S(1)}, u32[]{:S(2)}, u32[]{:S(2)}) async-start(bf16[4,400,128]{2,1,0:T(8,128)(2,1)} %pack.1), calls=%async_computation | async-start | bytes 819200 | tf_op jit(solution)/shard_map/all_to_all | solution.py:288
  13.4 0.7 copy-start.6
  15.4 0.8 copy-start.3
  15.4 0.8 copy-start.4
  15.4 0.8 copy-start.5
  24.6 7.5 %collective-permute-start.3 = (bf16[104,1536]{1,0:T(8,128)(2,1)S(1)}, bf16[104,1536]{1,0:T(8,128)(2,1)S(1)}, u32[]{:S(2)}, u32[]{:S(2)}) collective-permute-start(bf16[104,1536]{1,0:T(8,128)(2,1)S(1)} %shard_map.122), channel_id=1, source_target_pairs={{0,4},{4,0},{1,5},{5,1},{2,6},{6,2},{3,7},{7,3},{8,12},{12,8},{9,1... | collective-permute-start | bytes 958472 | tf_op jit(solution)/shard_map/ppermute | solution.py:352
  33.0 25.6 %all-to-all-start.1 = ((bf16[64,24,128]{2,1,0:T(8,128)(2,1)}), bf16[64,24,128]{2,1,0:T(8,128)(2,1)S(1)}, u32[]{:S(2)}, u32[]{:S(2)}) async-start(bf16[64,24,128]{2,1,0:T(8,128)(2,1)} %shard_map.123), calls=%async_computation.1 | async-start | bytes 786432 | tf_op jit(solution)/shard_map/all_to_all | solution.py:288
  78.0 31.7 %collective-permute-start.4 = (bf16[64,24,128]{2,1,0:T(8,128)(2,1)S(1)}, bf16[64,24,128]{2,1,0:T(8,128)(2,1)S(1)}, u32[]{:S(2)}, u32[]{:S(2)}) collective-permute-start(bf16[64,24,128]{2,1,0:T(8,128)(2,1)S(1)} %all_to_all.20.near), channel_id=1, source_target_pairs={{0,4},{4,0},{1,5},{5,1},{2,6},{6,2},{3,7},{7,3},{8,12},{12,8},{9,1... | collective-permute-start | bytes 1179656 | tf_op jit(solution)/shard_map/ppermute | solution.py:397
  85.1 25.8 %all-to-all-start.3 = ((bf16[8,4,1536]{2,1,0:T(4,128)(2,1)}), bf16[8,4,1536]{2,1,0:T(4,128)(2,1)S(1)}, u32[]{:S(2)}, u32[]{:S(2)}) async-start(bf16[8,4,1536]{2,1,0:T(4,128)(2,1)} %shard_map.125), calls=%async_computation.3 | async-start | bytes 196608 | tf_op jit(solution)/shard_map/all_to_all | solution.py:288
  88.4 20.6 %copy-start.1 = (bf16[1,1,320,128]{3,2,1,0:T(8,128)(2,1)S(1)}, bf16[1,1,320,128]{3,2,1,0:T(8,128)(2,1)}, u32[]{:S(2)}) copy-start(bf16[1,1,320,128]{3,2,1,0:T(8,128)(2,1)} %param.7) | copy-start | bytes 245764
  88.4 20.6 %copy-start.2 = (bf16[1,1,320,128]{3,2,1,0:T(8,128)(2,1)S(1)}, bf16[1,1,320,128]{3,2,1,0:T(8,128)(2,1)}, u32[]{:S(2)}) copy-start(bf16[1,1,320,128]{3,2,1,0:T(8,128)(2,1)} %param.8) | copy-start | bytes 245764
  89.7 14.6 %collective-permute-start = (bf16[400,128]{1,0:T(8,128)(2,1)S(1)}, bf16[400,128]{1,0:T(8,128)(2,1)S(1)}, u32[]{:S(2)}, u32[]{:S(2)}) collective-permute-start(bf16[400,128]{1,0:T(8,128)(2,1)S(1)} %get-tuple-element.25), channel_id=1, source_target_pairs={{0,1},{1,2},{2,3},{3,0},{4,5},{5,6},{6,7},{7,4},{8,9},{9,10},{10,1... | collective-permute-start | bytes 307208 | tf_op jit(solution)/shard_map/ppermute | solution.py:370
  93.9 10.5 %collective-permute-start.1 = (bf16[400,128]{1,0:T(8,128)(2,1)S(1)}, bf16[400,128]{1,0:T(8,128)(2,1)S(1)}, u32[]{:S(2)}, u32[]{:S(2)}) collective-permute-start(bf16[400,128]{1,0:T(8,128)(2,1)S(1)} %get-tuple-element.26), channel_id=1, source_target_pairs={{0,2},{1,3},{2,0},{3,1},{4,6},{5,7},{6,4},{7,5},{8,10},{9,11},{10,... | collective-permute-start | bytes 307208 | tf_op jit(solution)/shard_map/ppermute | solution.py:370
  99.1 9.9 %collective-permute-start.2 = (bf16[400,128]{1,0:T(8,128)(2,1)S(1)}, bf16[400,128]{1,0:T(8,128)(2,1)S(1)}, u32[]{:S(2)}, u32[]{:S(2)}) collective-permute-start(bf16[400,128]{1,0:T(8,128)(2,1)S(1)} %get-tuple-element.27), channel_id=1, source_target_pairs={{0,3},{1,0},{2,1},{3,2},{4,7},{5,4},{6,5},{7,6},{8,11},{9,8},{10,9... | collective-permute-start | bytes 307208 | tf_op jit(solution)/shard_map/ppermute | solution.py:370

commit v6 on v4

--- a/solution.py
+++ b/solution.py
@@ -199,11 +199,8 @@
     here = (row >= 0) & (row < cores * share) & (wide >= 0) & (row // share == owner % cores)
     here = here & (within // capacity == array) & (within % capacity == place)
     here = jnp.where(here, 1.0, 0.0).astype(bf16)
-    values = [received[chip].astype(f32) for chip in range(chips)]
-    grads = values[0]
-    for value in values[1:]:
-        grads = grads + value
-    picked = dot(jnp.concatenate(values, axis=0).astype(bf16), here, 1, 0)
+    grads = jnp.sum(received[...].astype(f32), axis=0)
+    picked = dot(rows_of(received), here, 1, 0)
     state = jnp.zeros((chunk, 3 * LANES), f32)
     for chip in range(chips):
         state = jnp.where(
@@ -226,9 +223,9 @@
         message[chip] = value.astype(bf16)
 
 
-def flat(messages):
+def rows_of(messages):
     chips, chunk, _ = messages.shape
-    return messages[...].astype(f32).reshape(chips * chunk, LANES)
+    return messages[...].reshape(chips * chunk, LANES)
 
 
 def unit(rows, first):
@@ -241,17 +238,17 @@
 
 def owned_body(near, message, *, quarter, capacity, strips):
     targets = message.shape[0]
-    turned = dot(unit(16, quarter), flat(near).astype(bf16), 1, 1)
+    turned = dot(unit(16, quarter), rows_of(near), 1, 1)
     for target in range(targets):
         first = target // strips * capacity
         message[target] = turned[first : first + capacity].astype(bf16)
 
 
 def collect_weight_body(core, near, far, new_weight, *, step):
-    ours, others = flat(near), flat(far)
+    ours, others = rows_of(near), rows_of(far)
     first = core[0] == 0
     rows = [jnp.where(first, ours, others)[:step], jnp.where(first, others, ours)[:step]]
-    rows = jnp.concatenate(rows, axis=0).astype(bf16)
+    rows = jnp.concatenate(rows, axis=0)
     new_weight[...] = dot(unit(new_weight.shape[0], 0), rows, 1, 1).astype(bf16)
 
 

time: 112 us -> 112 us (level)
  no operation moved by 1% of the time
where the time goes in v6:
time: 112 us
  starting transfers between devices  52.2 us (47%)
  waiting for transfers between devices  25.3 us (23%)
  blocking collectives  19 us (17%)
  Pallas kernels  10.4 us (9%)
  local copies, waits for them, and re-layouts  2.21 us (2%)
  other arithmetic  1.51 us (1%)
    all_to_all x3, starting transfers between devices, exchange(): return lax.all_to_all(value, axes, 0, 0, tiled=True)  25.7 us
    all_to_all x3, waiting for transfers between devices, exchange(): return lax.all_to_all(value, axes, 0, 0, tiled=True)  19.7 us
    all_to_all x1, blocking collectives, exchange(): return lax.all_to_all(value, axes, 0, 0, tiled=True)  19 us
    ppermute x3, starting transfers between devices, local(): returned.append(lax.ppermute(results[ahead], 'strip', pairs))  14.5 us
    ppermute x1, starting transfers between devices, local(): swapped = lax.ppermute(sent, 'core', swap)  6.29 us
    ppermute x1, starting transfers between devices, local(): far = lax.ppermute(near, 'core', swap)  5.76 us
    ppermute x3, waiting for transfers between devices, local(): returned.append(lax.ppermute(results[ahead], 'strip', pairs))  5.45 us
  transfers between devices with their start and end apart: 8, of which 5 were waited for; matrix products, arithmetic and copies ran while one was open for 2% of the time, Pallas kernels for 5%

profile of v6, /device:TPU:1, one launch (start us, length us, event | category | flops | bytes accessed | tf_op | source)
XLA Modules:
  0.0 111.5 jit_solution(6872835880223927717)
XLA Ops:
  0.6 1.7 %pack.1 = bf16[4,400,128]{2,1,0:T(8,128)(2,1)} custom-call(bf16[320,128]{1,0:T(8,128)(2,1)} %bitcast.10, bf16[320,128]{1,0:T(8,128)(2,1)} %bitcast.12), custom_call_target="tpu_custom_call" | custom-call | tf_op jit(solution)/shard_map/pack/pallas_call | solution.py:308
  2.4 11.0 %all-to-all-start = ((bf16[4,400,128]{2,1,0:T(8,128)(2,1)}), bf16[4,400,128]{2,1,0:T(8,128)(2,1)S(1)}, u32[]{:S(2)}, u32[]{:S(2)}) async-start(bf16[4,400,128]{2,1,0:T(8,128)(2,1)} %pack.1), calls=%async_computation | async-start | bytes 819200 | tf_op jit(solution)/shard_map/all_to_all | solution.py:284
  13.4 0.7 copy-done.6
  14.1 0.2 convert_reduce_fusion
  14.3 0.6 convert_reduce_fusion.1
  15.0 0.4 copy.17
  15.4 0.4 copy.18
  15.8 0.4 copy-done.3
  16.3 0.7 fusion.1.filled
  17.0 6.5 %all-to-all-done.gathered = bf16[4,400,128]{2,1,0:T(8,128)(2,1)S(1)} async-done(((bf16[4,400,128]{2,1,0:T(8,128)(2,1)}), bf16[4,400,128]{2,1,0:T(8,128)(2,1)S(1)}, u32[]{:S(2)}, u32[]{:S(2)}) %all-to-all-start) | async-done | bytes 409632 | tf_op jit(solution)/shard_map/all_to_all | solution.py:284
  23.5 1.1 shard_map.122
  24.6 6.3 %collective-permute-start.3 = (bf16[104,1536]{1,0:T(8,128)(2,1)S(1)}, bf16[104,1536]{1,0:T(8,128)(2,1)S(1)}, u32[]{:S(2)}, u32[]{:S(2)}) collective-permute-start(bf16[104,1536]{1,0:T(8,128)(2,1)S(1)} %shard_map.122), channel_id=1, source_target_pairs={{0,4},{4,0},{1,5},{5,1},{2,6},{6,2},{3,7},{7,3},{8,12},{12,8},{9,1... | collective-permute-start | bytes 958472 | tf_op jit(solution)/shard_map/ppermute | solution.py:348
  30.9 1.1 shard_map.121.kept
  31.9 0.1 collective-permute-done.3.received
  32.1 0.9 shard_map.123
  33.0 11.4 %all-to-all-start.1 = ((bf16[64,24,128]{2,1,0:T(8,128)(2,1)}), bf16[64,24,128]{2,1,0:T(8,128)(2,1)S(1)}, u32[]{:S(2)}, u32[]{:S(2)}) async-start(bf16[64,24,128]{2,1,0:T(8,128)(2,1)} %shard_map.123), calls=%async_computation.1 | async-start | bytes 786432 | tf_op jit(solution)/shard_map/all_to_all | solution.py:284
  44.4 13.2 %all-to-all-done.1.received = bf16[64,24,128]{2,1,0:T(8,128)(2,1)S(1)} async-done(((bf16[64,24,128]{2,1,0:T(8,128)(2,1)}), bf16[64,24,128]{2,1,0:T(8,128)(2,1)S(1)}, u32[]{:S(2)}, u32[]{:S(2)}) %all-to-all-start.1) | async-done | bytes 393248 | tf_op jit(solution)/shard_map/all_to_all | solution.py:284
  57.6 0.6 shard_map.124
  58.3 19.0 %all_to_all.20.near = bf16[64,24,128]{2,1,0:T(8,128)(2,1)S(1)} all-to-all(bf16[64,24,128]{2,1,0:T(8,128)(2,1)S(1)} %shard_map.124), channel_id=1, replica_groups=mesh['line'=8,'group'=8,'core'=2,'strip'=4] {'line','group'}, dimensions={0} | all-to-all | bytes 786432 | tf_op jit(solution)/shard_map/all_to_all | solution.py:284
  77.2 5.8 %collective-permute-start.4 = (bf16[64,24,128]{2,1,0:T(8,128)(2,1)S(1)}, bf16[64,24,128]{2,1,0:T(8,128)(2,1)S(1)}, u32[]{:S(2)}, u32[]{:S(2)}) collective-permute-start(bf16[64,24,128]{2,1,0:T(8,128)(2,1)S(1)} %all_to_all.20.near), channel_id=1, source_target_pairs={{0,4},{4,0},{1,5},{5,1},{2,6},{6,2},{3,7},{7,3},{8,12},{12,8},{9,1... | collective-permute-start | bytes 1179656 | tf_op jit(solution)/shard_map/ppermute | solution.py:390
  83.0 0.2 copy.19.turned
  83.2 0.9 shard_map.125
  84.1 3.3 %all-to-all-start.3 = ((bf16[8,4,1536]{2,1,0:T(4,128)(2,1)}), bf16[8,4,1536]{2,1,0:T(4,128)(2,1)S(1)}, u32[]{:S(2)}, u32[]{:S(2)}) async-start(bf16[8,4,1536]{2,1,0:T(4,128)(2,1)} %shard_map.125), calls=%async_computation.3 | async-start | bytes 196608 | tf_op jit(solution)/shard_map/all_to_all | solution.py:284
  87.5 1.3 %shard_map.119 = (bf16[400,128]{1,0:T(8,128)(2,1)S(1)}, bf16[400,128]{1,0:T(8,128)(2,1)S(1)}, bf16[400,128]{1,0:T(8,128)(2,1)S(1)}, bf16[400,128]{1,0:T(8,128)(2,1)S(1)}) custom-call(s32[1]{0:T(128)} %bitcast.strip, bf16[4,400,128]{2,1,0:T(8,128)(2,1)S(1)} %all-to-all-done.gathered, bf16[4,80,128]{2,1,0:T(8,128)(2,1)S(1)} %constant_dynamic-slice_fusion.residual, ...), custom_call_target="tpu_custom_call" | custom-call | tf_op jit(solution)/shard_map/pallas_call | solution.py:351
  88.8 4.1 %collective-permute-start = (bf16[400,128]{1,0:T(8,128)(2,1)S(1)}, bf16[400,128]{1,0:T(8,128)(2,1)S(1)}, u32[]{:S(2)}, u32[]{:S(2)}) collective-permute-start(bf16[400,128]{1,0:T(8,128)(2,1)S(1)} %get-tuple-element.25), channel_id=1, source_target_pairs={{0,1},{1,2},{2,3},{3,0},{4,5},{5,6},{6,7},{7,4},{8,9},{9,10},{10,1... | collective-permute-start | bytes 307208 | tf_op jit(solution)/shard_map/ppermute | solution.py:366
  92.9 5.2 %collective-permute-start.1 = (bf16[400,128]{1,0:T(8,128)(2,1)S(1)}, bf16[400,128]{1,0:T(8,128)(2,1)S(1)}, u32[]{:S(2)}, u32[]{:S(2)}) collective-permute-start(bf16[400,128]{1,0:T(8,128)(2,1)S(1)} %get-tuple-element.26), channel_id=1, source_target_pairs={{0,2},{1,3},{2,0},{3,1},{4,6},{5,7},{6,4},{7,5},{8,10},{9,11},{10,... | collective-permute-start | bytes 307208 | tf_op jit(solution)/shard_map/ppermute | solution.py:366
  98.1 5.2 %collective-permute-start.2 = (bf16[400,128]{1,0:T(8,128)(2,1)S(1)}, bf16[400,128]{1,0:T(8,128)(2,1)S(1)}, u32[]{:S(2)}, u32[]{:S(2)}) collective-permute-start(bf16[400,128]{1,0:T(8,128)(2,1)S(1)} %get-tuple-element.27), channel_id=1, source_target_pairs={{0,3},{1,0},{2,1},{3,2},{4,7},{5,4},{6,5},{7,6},{8,11},{9,8},{10,9... | collective-permute-start | bytes 307208 | tf_op jit(solution)/shard_map/ppermute | solution.py:366
  103.4 2.3 %collective-permute-done.1.pieces_2_ = bf16[400,128]{1,0:T(8,128)(2,1)S(1)} collective-permute-done((bf16[400,128]{1,0:T(8,128)(2,1)S(1)}, bf16[400,128]{1,0:T(8,128)(2,1)S(1)}, u32[]{:S(2)}, u32[]{:S(2)}) %collective-permute-start.1) | collective-permute-done | bytes 102432 | tf_op jit(solution)/shard_map/ppermute | solution.py:366
  105.6 3.2 %collective-permute-done.2.pieces_3_ = bf16[400,128]{1,0:T(8,128)(2,1)S(1)} collective-permute-done((bf16[400,128]{1,0:T(8,128)(2,1)S(1)}, bf16[400,128]{1,0:T(8,128)(2,1)S(1)}, u32[]{:S(2)}, u32[]{:S(2)}) %collective-permute-start.2) | collective-permute-done | bytes 102432 | tf_op jit(solution)/shard_map/ppermute | solution.py:366
  108.8 0.8 shard_map.120
  109.6 1.2 %shard_map.126 = bf16[80,2880]{1,0:T(8,128)(2,1)} custom-call(s32[1]{0:T(128)} %bitcast.8.core, bf16[64,24,128]{2,1,0:T(8,128)(2,1)S(1)} %all_to_all.20.near, bf16[64,24,128]{2,1,0:T(8,128)(2,1)S(1)} %collective-permute-done.4.far), custom_call_target="tpu_custom_call" | custom-call | tf_op jit(solution)/shard_map/pallas_call | solution.py:396
  110.7 0.8 shard_map.127
  (19 shorter events, 0.3 us)
Async XLA Ops:
  2.4 12.6 %copy-start = (bf16[80,2880]{1,0:T(8,128)(2,1)S(1)}, bf16[80,2880]{1,0:T(8,128)(2,1)}, u32[]{:S(2)}) copy-start(bf16[80,2880]{1,0:T(8,128)(2,1)} %weight.1) | copy-start | bytes 1382404
  2.4 21.1 %all-to-all-start = ((bf16[4,400,128]{2,1,0:T(8,128)(2,1)}), bf16[4,400,128]{2,1,0:T(8,128)(2,1)S(1)}, u32[]{:S(2)}, u32[]{:S(2)}) async-start(bf16[4,400,128]{2,1,0:T(8,128)(2,1)} %pack.1), calls=%async_computation | async-start | bytes 819200 | tf_op jit(solution)/shard_map/all_to_all | solution.py:284
  13.4 0.7 copy-start.6
  15.4 0.8 copy-start.3
  15.4 0.8 copy-start.4
  15.4 0.8 copy-start.5
  24.6 7.5 %collective-permute-start.3 = (bf16[104,1536]{1,0:T(8,128)(2,1)S(1)}, bf16[104,1536]{1,0:T(8,128)(2,1)S(1)}, u32[]{:S(2)}, u32[]{:S(2)}) collective-permute-start(bf16[104,1536]{1,0:T(8,128)(2,1)S(1)} %shard_map.122), channel_id=1, source_target_pairs={{0,4},{4,0},{1,5},{5,1},{2,6},{6,2},{3,7},{7,3},{8,12},{12,8},{9,1... | collective-permute-start | bytes 958472 | tf_op jit(solution)/shard_map/ppermute | solution.py:348
  33.0 24.6 %all-to-all-start.1 = ((bf16[64,24,128]{2,1,0:T(8,128)(2,1)}), bf16[64,24,128]{2,1,0:T(8,128)(2,1)S(1)}, u32[]{:S(2)}, u32[]{:S(2)}) async-start(bf16[64,24,128]{2,1,0:T(8,128)(2,1)} %shard_map.123), calls=%async_computation.1 | async-start | bytes 786432 | tf_op jit(solution)/shard_map/all_to_all | solution.py:284
  77.2 32.3 %collective-permute-start.4 = (bf16[64,24,128]{2,1,0:T(8,128)(2,1)S(1)}, bf16[64,24,128]{2,1,0:T(8,128)(2,1)S(1)}, u32[]{:S(2)}, u32[]{:S(2)}) collective-permute-start(bf16[64,24,128]{2,1,0:T(8,128)(2,1)S(1)} %all_to_all.20.near), channel_id=1, source_target_pairs={{0,4},{4,0},{1,5},{5,1},{2,6},{6,2},{3,7},{7,3},{8,12},{12,8},{9,1... | collective-permute-start | bytes 1179656 | tf_op jit(solution)/shard_map/ppermute | solution.py:390
  84.1 26.7 %all-to-all-start.3 = ((bf16[8,4,1536]{2,1,0:T(4,128)(2,1)}), bf16[8,4,1536]{2,1,0:T(4,128)(2,1)S(1)}, u32[]{:S(2)}, u32[]{:S(2)}) async-start(bf16[8,4,1536]{2,1,0:T(4,128)(2,1)} %shard_map.125), calls=%async_computation.3 | async-start | bytes 196608 | tf_op jit(solution)/shard_map/all_to_all | solution.py:284
  87.4 21.4 %copy-start.1 = (bf16[1,1,320,128]{3,2,1,0:T(8,128)(2,1)S(1)}, bf16[1,1,320,128]{3,2,1,0:T(8,128)(2,1)}, u32[]{:S(2)}) copy-start(bf16[1,1,320,128]{3,2,1,0:T(8,128)(2,1)} %param.7) | copy-start | bytes 245764
  87.4 21.4 %copy-start.2 = (bf16[1,1,320,128]{3,2,1,0:T(8,128)(2,1)S(1)}, bf16[1,1,320,128]{3,2,1,0:T(8,128)(2,1)}, u32[]{:S(2)}) copy-start(bf16[1,1,320,128]{3,2,1,0:T(8,128)(2,1)} %param.8) | copy-start | bytes 245764
  88.8 14.6 %collective-permute-start = (bf16[400,128]{1,0:T(8,128)(2,1)S(1)}, bf16[400,128]{1,0:T(8,128)(2,1)S(1)}, u32[]{:S(2)}, u32[]{:S(2)}) collective-permute-start(bf16[400,128]{1,0:T(8,128)(2,1)S(1)} %get-tuple-element.25), channel_id=1, source_target_pairs={{0,1},{1,2},{2,3},{3,0},{4,5},{5,6},{6,7},{7,4},{8,9},{9,10},{10,1... | collective-permute-start | bytes 307208 | tf_op jit(solution)/shard_map/ppermute | solution.py:366
  92.9 12.7 %collective-permute-start.1 = (bf16[400,128]{1,0:T(8,128)(2,1)S(1)}, bf16[400,128]{1,0:T(8,128)(2,1)S(1)}, u32[]{:S(2)}, u32[]{:S(2)}) collective-permute-start(bf16[400,128]{1,0:T(8,128)(2,1)S(1)} %get-tuple-element.26), channel_id=1, source_target_pairs={{0,2},{1,3},{2,0},{3,1},{4,6},{5,7},{6,4},{7,5},{8,10},{9,11},{10,... | collective-permute-start | bytes 307208 | tf_op jit(solution)/shard_map/ppermute | solution.py:366
  98.1 10.7 %collective-permute-start.2 = (bf16[400,128]{1,0:T(8,128)(2,1)S(1)}, bf16[400,128]{1,0:T(8,128)(2,1)S(1)}, u32[]{:S(2)}, u32[]{:S(2)}) collective-permute-start(bf16[400,128]{1,0:T(8,128)(2,1)S(1)} %get-tuple-element.27), channel_id=1, source_target_pairs={{0,3},{1,0},{2,1},{3,2},{4,7},{5,4},{6,5},{7,6},{8,11},{9,8},{10,9... | collective-permute-start | bytes 307208 | tf_op jit(solution)/shard_map/ppermute | solution.py:366
